TPU v7x, 32 devices: a whole 2x2x4 slice. The times are simulated.
32 devices in a mesh: dp: 16 (over z, y, x), mp: 2 (over core).
Axes of the slice: x: 2, y: 2, z: 4, core: 2. Of those that a mesh axis runs over, the one named last changes fastest.
Arguments:
- inputs: bfloat16 [16, 1024, 768], P('dp'), may hold values from -6 to 6
- time_embed: float32 [16, 768], P('dp'), may hold values from -3 to 3
- targets: bfloat16 [16, 1024, 768], P('dp'), may hold values from -6 to 6
- timesteps: int32 [16], P('dp'), may hold values from 0 to 1999
- ln1_gain: float32 [768], replicated, may hold values from 0.1 to 1.9
- ln1_bias: float32 [768], replicated, may hold values from -0.1 to 0.1
- qkv_weight: bfloat16 [768, 3, 768], P(None, None, 'mp'), may hold values from -0.21875 to 0.21875
- qv_bias: float32 [2, 768], P(None, 'mp'), may hold values from -3 to 3
- out_weight: bfloat16 [768, 768], P('mp'), may hold values from -1.75 to 1.75
- out_bias: float32 [768], replicated, may hold values from -0.25 to 0.25
- ln2_gain: float32 [768], replicated, may hold values from 0.1 to 1.9
- ln2_bias: float32 [768], replicated, may hold values from -0.5 to 0.5
- up_weight: bfloat16 [768, 3072], P(None, 'mp'), may hold values from -0.21875 to 0.21875
- up_bias: float32 [3072], P('mp'), may hold values from -0.25 to 0.25
- down_weight: bfloat16 [3072, 768], P('mp'), may hold values from -0.109375 to 0.109375
- down_bias: float32 [768], replicated, may hold values from -0.25 to 0.25
Outputs:
- out_act: bfloat16 [16, 1024, 768], P('dp')
- grad_input: float32 [16, 1024, 768], P('dp')
- grad_time: float32 [16, 768], P('dp')
- grad_ln1_gain: float32 [768], replicated
- grad_ln1_bias: float32 [768], replicated
- grad_qkv: float32 [768, 3, 768], P('dp', None, 'mp')
- grad_qv_bias: float32 [2, 768], P(None, 'mp')
- grad_out: float32 [768, 768], P('mp', 'dp')
- grad_out_bias: float32 [768], replicated
- grad_ln2_gain: float32 [768], replicated
- grad_ln2_bias: float32 [768], replicated
- grad_up: float32 [768, 3072], P('dp', 'mp')
- grad_up_bias: float32 [3072], P('mp')
- grad_down: float32 [3072, 768], P('mp', 'dp')
- grad_down_bias: float32 [768], replicated
- bucket_counts: int32 [4], replicated
All inputs are finite; a program needn't handle non-finite values.
Results may differ from a plain program's by a relative error of at most 0.0055.
Values sent between devices are 32-bit elements; how exact they have to be, the bound alone decides.
No kernel may reach another device: no remote copies, remote signals or barrier semaphores. Data moves between devices by JAX's collectives and lax.ppermute only.
A program may use at most 192 MiB of HBM per device.

v0:
```python
import math

import jax
import jax.numpy as jnp
from jax import lax
from jax.sharding import PartitionSpec as P

HD = 64
NSTEPS = 2000
NB = 4


epsilon = 1e-05


def normalize(source, scaling, offset):
    row_mean = jnp.mean(source, axis=-1, keepdims=True)
    centred = source - row_mean
    variance = jnp.mean(centred * centred, axis=-1, keepdims=True)
    inv_std = lax.rsqrt(variance + epsilon)
    normed = centred * inv_std
    return (normed * scaling + offset, normed, inv_std)


def norm_back(upstream, normed, inv_std, scaling):
    scaled = upstream * scaling
    inner_part = (
        scaled
        - jnp.mean(scaled, axis=-1, keepdims=True)
        - normed * jnp.mean(scaled * normed, axis=-1, keepdims=True)
    )
    return (inv_std * inner_part, jnp.sum(upstream * normed, axis=0), jnp.sum(upstream, axis=0))


def local(
    inputs,
    time_embed,
    targets,
    timesteps,
    ln1_gain,
    ln1_bias,
    qkv_weight,
    qv_bias,
    out_weight,
    out_bias,
    ln2_gain,
    ln2_bias,
    up_weight,
    up_bias,
    down_weight,
    down_bias,
):
    seq_count, length, model_width = inputs.shape
    tok_rows = seq_count * length
    local_width = qkv_weight.shape[2]
    heads_local = local_width // HD
    score_scale = 1.0 / math.sqrt(HD)
    head_shape = (seq_count, length, heads_local, HD)
    buckets = (
        (timesteps >= NSTEPS // 64).astype(jnp.int32)
        + (timesteps >= NSTEPS // 16).astype(jnp.int32)
        + (timesteps >= NSTEPS // 4).astype(jnp.int32)
    )
    one_hot = buckets[:, None] == jnp.arange(NB, dtype=jnp.int32)[None, :]
    bucket_counts = lax.psum(jnp.sum(one_hot.astype(jnp.int32), axis=0), "dp")
    floors = jnp.maximum(bucket_counts, 1).astype(jnp.float32)
    total_seqs = seq_count * lax.axis_size("dp")
    seq_weight = total_seqs / (NB * jnp.sum(jnp.where(one_hot, floors[None, :], 0.0), axis=1))
    residual = (inputs.astype(jnp.float32) + time_embed[:, None, :]).reshape(tok_rows, model_width)
    first_out, first_normed, first_inv = normalize(residual, ln1_gain, ln1_bias)
    attn_in = first_out.astype(jnp.bfloat16)
    projected = jnp.einsum("td,dsk->tsk", attn_in, qkv_weight, preferred_element_type=jnp.float32)
    queries = (projected[:, 0] + qv_bias[0]).astype(jnp.bfloat16).reshape(head_shape)
    keyset = projected[:, 1].astype(jnp.bfloat16).reshape(head_shape)
    values = (projected[:, 2] + qv_bias[1]).astype(jnp.bfloat16).reshape(head_shape)
    span_rows = min(512, length)
    span_count = length // span_rows

    def scores_of(position):
        query_piece = queries[:, position * span_rows : (position + 1) * span_rows]
        scores = (
            jnp.einsum("bqhe,bkhe->bhqk", query_piece, keyset, preferred_element_type=jnp.float32)
            * score_scale
        )
        return (query_piece, scores)

    mixed_parts = []
    log_totals = []
    for position in range(span_count):
        query_piece, scores = scores_of(position)
        row_max = jnp.max(scores, axis=-1, keepdims=True)
        expo_vals = jnp.exp(scores - row_max)
        row_total = jnp.sum(expo_vals, axis=-1, keepdims=True)
        attn_probs = expo_vals / row_total
        log_totals.append(row_max + jnp.log(row_total))
        mixed_parts.append(
            jnp.einsum(
                "bhqk,bkhe->bqhe",
                attn_probs.astype(jnp.bfloat16),
                values,
                preferred_element_type=jnp.float32,
            )
        )
    mixed_heads = (
        jnp.concatenate(mixed_parts, axis=1).reshape(tok_rows, local_width).astype(jnp.bfloat16)
    )
    attn_sum = lax.psum(jnp.dot(mixed_heads, out_weight, preferred_element_type=jnp.float32), "mp")
    mid_state = residual + attn_sum + out_bias
    second_out, second_normed, second_inv = normalize(mid_state, ln2_gain, ln2_bias)
    ffn_in = second_out.astype(jnp.bfloat16)
    preact = jnp.dot(ffn_in, up_weight, preferred_element_type=jnp.float32) + up_bias
    gelu_value, gelu_back = jax.vjp(
        lambda inner_arg: jax.nn.gelu(inner_arg, approximate=False), preact
    )
    activated = gelu_value.astype(jnp.bfloat16)
    ffn_sum = lax.psum(jnp.dot(activated, down_weight, preferred_element_type=jnp.float32), "mp")
    final_state = mid_state + ffn_sum + down_bias
    out_act = final_state.astype(jnp.bfloat16).reshape(seq_count, length, model_width)
    misfit = final_state.reshape(seq_count, length, model_width) - targets.astype(jnp.float32)
    out_grad = (misfit * seq_weight[:, None, None]).reshape(tok_rows, model_width)
    out_grad_low = out_grad.astype(jnp.bfloat16)
    grad_down = jnp.einsum("tf,td->fd", activated, out_grad_low, preferred_element_type=jnp.float32)
    pre_grad = gelu_back(
        jnp.einsum("td,fd->tf", out_grad_low, down_weight, preferred_element_type=jnp.float32)
    )[0]
    pre_grad_low = pre_grad.astype(jnp.bfloat16)
    grad_up = jnp.einsum("td,tf->df", ffn_in, pre_grad_low, preferred_element_type=jnp.float32)
    ffn_grad = lax.psum(
        jnp.einsum("tf,df->td", pre_grad_low, up_weight, preferred_element_type=jnp.float32), "mp"
    )
    mid_back, grad_ln2_gain, grad_ln2_bias = norm_back(
        ffn_grad, second_normed, second_inv, ln2_gain
    )
    mid_grad = out_grad + mid_back
    mid_grad_low = mid_grad.astype(jnp.bfloat16)
    grad_out = jnp.einsum(
        "tk,td->kd", mixed_heads, mid_grad_low, preferred_element_type=jnp.float32
    )
    mixed_grad = (
        jnp.einsum("td,kd->tk", mid_grad_low, out_weight, preferred_element_type=jnp.float32)
        .astype(jnp.bfloat16)
        .reshape(head_shape)
    )
    key_grad = jnp.zeros(head_shape, jnp.float32)
    value_grad = jnp.zeros(head_shape, jnp.float32)
    query_parts = []
    for position in range(span_count):
        query_piece, scores = scores_of(position)
        attn_probs = jnp.exp(scores - log_totals[position])
        grad_piece = mixed_grad[:, position * span_rows : (position + 1) * span_rows]
        prob_grad = jnp.einsum(
            "bqhe,bkhe->bhqk", grad_piece, values, preferred_element_type=jnp.float32
        )
        row_dot = jnp.sum(prob_grad * attn_probs, axis=-1, keepdims=True)
        score_grad = (attn_probs * (prob_grad - row_dot)).astype(jnp.bfloat16)
        query_parts.append(
            jnp.einsum("bhqk,bkhe->bqhe", score_grad, keyset, preferred_element_type=jnp.float32)
            * score_scale
        )
        key_grad = (
            key_grad
            + jnp.einsum(
                "bhqk,bqhe->bkhe", score_grad, query_piece, preferred_element_type=jnp.float32
            )
            * score_scale
        )
        value_grad = value_grad + jnp.einsum(
            "bhqk,bqhe->bkhe",
            attn_probs.astype(jnp.bfloat16),
            grad_piece,
            preferred_element_type=jnp.float32,
        )
    query_grad = jnp.concatenate(query_parts, axis=1).reshape(tok_rows, local_width)
    key_flat = key_grad.reshape(tok_rows, local_width)
    value_flat = value_grad.reshape(tok_rows, local_width)
    qv_bias_grad = jnp.stack([jnp.sum(query_grad, axis=0), jnp.sum(value_flat, axis=0)])
    proj_grad = jnp.stack([query_grad, key_flat, value_flat], axis=1).astype(jnp.bfloat16)
    grad_qkv = jnp.einsum("td,tsk->dsk", attn_in, proj_grad, preferred_element_type=jnp.float32)
    attn_grad = lax.psum(
        jnp.einsum("tsk,dsk->td", proj_grad, qkv_weight, preferred_element_type=jnp.float32), "mp"
    )
    input_back, grad_ln1_gain, grad_ln1_bias = norm_back(
        attn_grad, first_normed, first_inv, ln1_gain
    )
    input_grad = (mid_grad + input_back).reshape(seq_count, length, model_width)
    grad_time = jnp.sum(input_grad, axis=1)
    small_sums = lax.psum(
        (
            grad_ln1_gain,
            grad_ln1_bias,
            qv_bias_grad,
            jnp.sum(mid_grad, axis=0),
            grad_ln2_gain,
            grad_ln2_bias,
            jnp.sum(pre_grad, axis=0),
            jnp.sum(out_grad, axis=0),
        ),
        "dp",
    )
    grad_qkv_part, grad_out_part, grad_up_part, grad_down_part = (
        lax.psum_scatter(grad_qkv, "dp", scatter_dimension=0, tiled=True),
        lax.psum_scatter(grad_out, "dp", scatter_dimension=1, tiled=True),
        lax.psum_scatter(grad_up, "dp", scatter_dimension=0, tiled=True),
        lax.psum_scatter(grad_down, "dp", scatter_dimension=1, tiled=True),
    )
    return (
        out_act,
        input_grad,
        grad_time,
        small_sums[0],
        small_sums[1],
        grad_qkv_part,
        small_sums[2],
        grad_out_part,
        small_sums[3],
        small_sums[4],
        small_sums[5],
        grad_up_part,
        small_sums[6],
        grad_down_part,
        small_sums[7],
        bucket_counts,
    )


def solution(mesh):
    in_specs = (
        P("dp", None, None),
        P("dp", None),
        P("dp", None, None),
        P("dp"),
        P(),
        P(),
        P(None, None, "mp"),
        P(None, "mp"),
        P("mp", None),
        P(),
        P(),
        P(),
        P(None, "mp"),
        P("mp"),
        P("mp", None),
        P(),
    )
    out_specs = (
        P("dp", None, None),
        P("dp", None, None),
        P("dp", None),
        P(),
        P(),
        P("dp", None, "mp"),
        P(None, "mp"),
        P("mp", "dp"),
        P(),
        P(),
        P(),
        P("dp", "mp"),
        P("mp"),
        P("mp", "dp"),
        P(),
        P(),
    )
    return jax.shard_map(local, mesh=mesh, in_specs=in_specs, out_specs=out_specs, check_vma=False)
```

profile of v0, /device:TPU:0, one launch (start us, length us, event | category | flops | bytes accessed | tf_op | source)
XLA Modules:
  0.0 830.2 jit_solution(15095251997524434872)
XLA Ops:
  7.3 0.8 reduce.22
  8.1 1.9 fusion.22
  10.1 2.1 multiply_reduce_fusion.9
  12.2 3.8 fusion.57
  16.2 1.9 fusion.69
  18.2 1.6 add_convert_fusion.2
  19.8 6.4 multiply_reduce_fusion.2
  26.2 6.3 multiply_reduce_fusion.3
  32.6 1.7 add_convert_fusion.3
  34.3 7.5 fusion.1
  41.8 3.6 fusion.37
  45.5 2.8 fusion
  48.3 3.6 fusion.36
  52.0 0.9 copy-done.13
  52.9 2.7 fusion.78
  55.7 26.0 %all-reduce.6.cloned.1.call-done = f32[1024,768]{1,0:T(8,128)} async-done(((f32[1024,768]{1,0:T(8,128)}), f32[1024,768]{1,0:T(8,128)}) %all-reduce.6.cloned.1.call-update) | async-done | bytes 3145744 | tf_op jit(solution)/shard_map/psum | solution.py:107
  81.7 2.9 fusion.67
  84.7 0.5 multiply_reduce_fusion.8
  85.5 17.6 %multiply_convert_fusion.2 = (bf16[1024,1536]{1,0:T(8,128)(2,1)S(1)}, f32[1024,1536]{1,0:T(8,128)}, f32[1024,1536]{1,0:T(8,128)}) fusion(f32[1536]{0:T(1024)S(1)} %copy-done.48, bf16[768,1536]{1,0:T(8,128)(2,1)S(1)} %copy-done, f32[1024,768]{1,0:T(8,128)S(1)} %get-tuple-element.43, f32[768]{0:T(1024)S(1)} %copy-done.49, f32[768]{0:T(1024)S(1)} %copy-done.39, ...), kind=kOutput, calls=%fused_computation.23 | convolution fusion | flops 2523660288 | bytes 21254144 | tf_op jit(solution)/shard_map/dot_general | solution.py:111
  103.0 1.6 copy-done.54
  104.7 4.3 fusion.79
  109.7 14.7 %psum.93 = s32[4]{0:T(128)S(1)} all-reduce(s32[4]{0:T(128)S(1)} %compare_convert_fusion), channel_id=1, replica_groups=mesh['dp'=16,'mp'=2] {'dp'}, use_global_device_ids=true, to_apply=%region_10.11 | all-reduce | flops 4 | bytes 32 | tf_op jit(solution)/shard_map/psum | solution.py:65
  124.4 0.6 fusion.49
  125.7 7.8 all-reduce.8.cloned.1.call-done
  133.5 4.7 fusion.62
  138.3 9.3 %fusion.72 = (f32[1536]{0:T(1024)}, bf16[1024,1536]{1,0:T(8,128)(2,1)S(1)}) fusion(f32[1024,1536]{1,0:T(8,128)} %get-tuple-element.41, bf16[1536,768]{1,0:T(8,128)(2,1)S(1)} %copy-done.47, f32[1024,1536]{1,0:T(8,128)} %get-tuple-element.55, f32[1536]{0:T(1024)S(1)} %copy-done.48, f32[1,1024,768]{2,1,0:T(8,128)S(1)} %get-tuple-element.35), kind=kOutput, calls=%fused_computation.136 | convolution fusion | flops 2441083392 | bytes 21245952 | tf_op jit(solution)/shard_map/td,fd->tf/dot_general | solution.py:124
  147.5 1.6 copy-done.55
  149.2 4.4 fusion.27
  153.7 24.4 %all-reduce.10.cloned.1.call-done = f32[1024,768]{1,0:T(8,128)} async-done(((f32[1024,768]{1,0:T(8,128)}), f32[1024,768]{1,0:T(8,128)}) %all-reduce.10.cloned.1.call-update) | async-done | bytes 3145744 | tf_op jit(solution)/shard_map/psum | solution.py:128
  178.1 4.7 multiply_reduce_fusion.4
  182.9 7.2 fusion.64
  190.2 0.8 convolution_convert_fusion
  191.0 0.9 copy-done.4
  191.9 3.5 fusion.4
  195.4 7.0 multiply_reduce_fusion
  202.4 6.3 multiply_reduce_fusion.1
  208.8 6.5 multiply_convert_fusion.1
  215.3 2.7 fusion.71
  218.1 1.2 fusion.44
  219.3 0.4 copy-done.17
  219.7 3.7 bitcast_convert_fusion.1
  223.4 2.3 copy.35
  225.7 9.7 %multiply_convert_fusion = bf16[6,512,1024]{2,1,0:T(8,128)(2,1)S(1)} fusion(f32[6,512,1024]{2,1,0:T(8,128)} %get-tuple-element.61, f32[6,512,1024]{2,1,0:T(8,128)} %get-tuple-element.52, f32[6,512]{1,0:T(8,128)} %get-tuple-element.60, f32[6,512]{1,0:T(8,128)} %copy-done.22), kind=kLoop, calls=%fused_computation | loop fusion | flops 15728640 | bytes 31481856 | tf_op jit(solution)/shard_map/convert_element_type | solution.py:155
  235.4 2.8 fusion.70
  238.2 1.3 multiply_convert_fusion.3
  239.8 1.1 pad_maximum_fusion.4
  240.9 0.4 copy.33
  241.3 5.6 convolution_bitcast_fusion
  247.0 1.1 copy-done.14
  248.1 3.9 fusion.41
  252.1 8.4 %fusion.73 = f32[1536,768]{0,1:T(8,128)} fusion(bf16[1024,1536]{1,0:T(8,128)(2,1)} %copy-done.54, f32[1,1024,768]{2,1,0:T(8,128)} %copy-done.9), kind=kOutput, calls=%fused_computation.137 | convolution fusion | flops 2415919104 | bytes 11010048 | tf_op jit(solution)/shard_map/tf,td->fd/dot_general | solution.py:122
  260.6 0.6 copy-done.28
  261.2 8.2 fusion.25
  269.7 1.1 copy-done.6
  270.8 5.4 fusion.38
  276.3 1.6 bitcast_reduce_fusion
  278.1 3.3 multiply_reduce_fusion.5
  281.5 4.3 fusion.65
  285.8 0.6 reduce_sum.243
  286.4 77.8 %all-reduce = (f32[768]{0:T(1024)}, f32[768]{0:T(1024)}, f32[2,384]{1,0:T(2,128)}, f32[768]{0:T(1024)}, f32[768]{0:T(1024)}, /*index=5*/f32[768]{0:T(1024)}, f32[1536]{0:T(1024)}, f32[768]{0:T(1024)}) all-reduce(f32[768]{0:T(1024)S(1)} %get-tuple-element.18, f32[768]{0:T(1024)S(1)} %get-tuple-element.23, ...), channel_id=1, replica_groups=mesh['dp'=16,'mp'=2] {'dp'}, use_global_device_ids=true, to_apply=%region_22.23 | all-reduce | flops 6912 | bytes 55296 | tf_op jit(solution)/shard_map/psum | solution.py:187
  364.2 37.3 %reduce-scatter.7.cloned.1.call-done = f32[384,48]{0,1:T(8,128)} async-done(((f32[384,768]{0,1:T(8,128)}), f32[384,48]{0,1:T(8,128)}) %reduce-scatter.7.cloned.1.call-update) | async-done | bytes 73744 | tf_op jit(solution)/shard_map/reduce_scatter | solution.py:202
  401.5 141.1 %reduce-scatter.11.cloned.1.call-done = f32[1536,48]{0,1:T(8,128)} async-done(((f32[1536,768]{0,1:T(8,128)}), f32[1536,48]{0,1:T(8,128)}) %reduce-scatter.11.cloned.1.call-update) | async-done | bytes 294928 | tf_op jit(solution)/shard_map/reduce_scatter | solution.py:204
  542.7 142.4 %reduce-scatter.9.cloned.1.call-done = f32[48,1536]{1,0:T(8,128)} async-done(((f32[768,1536]{1,0:T(8,128)}), f32[48,1536]{1,0:T(8,128)}) %reduce-scatter.9.cloned.1.call-update) | async-done | bytes 294928 | tf_op jit(solution)/shard_map/reduce_scatter | solution.py:203
  685.1 138.0 %reduce-scatter.5.cloned.1.call-done = f32[48,3,384]{2,0,1:T(8,128)} async-done(((f32[768,3,384]{2,0,1:T(8,128)}), f32[48,3,384]{2,0,1:T(8,128)}) %reduce-scatter.5.cloned.1.call-update) | async-done | bytes 221200 | tf_op jit(solution)/shard_map/reduce_scatter | solution.py:201
  (162 shorter events, 2.2 us)
Async XLA Ops:
  7.2 78.0 %copy-start = (bf16[768,1536]{1,0:T(8,128)(2,1)S(1)}, bf16[768,1536]{1,0:T(8,128)(2,1)}, u32[]{:S(2)}) copy-start(bf16[768,1536]{1,0:T(8,128)(2,1)} %param.28) | copy-start | bytes 7077892
  7.2 4.9 copy-start.34
  7.2 4.9 copy-start.51
  7.2 74.5 %all-reduce.6.cloned.1.call-start = ((), (), s32[]{:S(2)}) async-start(), calls=%async_computation.4 | async-start | bytes 6291456 | tf_op jit(solution)/shard_map/psum | solution.py:107
  8.1 73.6 %copy-start.23 = (f32[768]{0:T(1024)}, f32[768]{0:T(1024)S(1)}, u32[]{:S(2)}) copy-start(f32[768]{0:T(1024)S(1)} %reduce.22) | copy-start | bytes 9220
  8.1 4.0 copy-start.5
  10.1 6.0 copy-start.25
  12.2 3.9 copy-start.29
  16.2 10.0 %copy-start.7 = (bf16[1024,1,384]{0,2,1:T(8,128)(2,1)}, bf16[1024,1,384]{0,2,1:T(8,128)(2,1)S(1)}, u32[]{:S(2)}) copy-start(bf16[1024,1,384]{0,2,1:T(8,128)(2,1)S(1)} %slice.61) | copy-start | bytes 2359300
  16.2 1.9 copy-start.45
  19.7 6.4 copy-start.11
  32.6 9.2 %copy-start.2 = (f32[6,512,1024]{2,1,0:T(8,128)S(1)}, f32[6,512,1024]{2,1,0:T(8,128)}, u32[]{:S(2)}) copy-start(f32[6,512,1024]{2,1,0:T(8,128)} %get-tuple-element.52) | copy-start | bytes 37748740
  34.3 11.2 %slice-start = ((s8[12582912]{0:T(1024)(128)(4,1)}), s8[4194304]{0:T(1024)(128)(4,1)S(1)}, s32[]{:S(2)}) async-start(s8[12582912]{0:T(1024)(128)(4,1)} %bitcast.150), calls=%async_computation.12 | async-start | bytes 8388608
  41.8 3.7 slice-start.1
  41.8 3.7 slice-start.2
  48.3 4.6 copy-start.18
  52.9 28.8 %copy-start.44 = (f32[768]{0:T(1024)S(1)}, f32[768]{0:T(1024)}, u32[]{:S(2)}) copy-start(f32[768]{0:T(1024)} %param.25) | copy-start | bytes 9220
  55.6 77.9 %all-reduce.8.cloned.1.call-start = ((), (), s32[]{:S(2)}) async-start(), calls=%async_computation.5 | async-start | bytes 6291456 | tf_op jit(solution)/shard_map/psum | solution.py:116
  84.6 18.4 %copy-start.3 = (f32[1024,768]{1,0:T(8,128)}, f32[1024,768]{1,0:T(8,128)S(1)}, u32[]{:S(2)}) copy-start(f32[1024,768]{1,0:T(8,128)S(1)} %get-tuple-element.43) | copy-start | bytes 9437188
  84.7 98.2 %copy-start.27 = (f32[1024]{0:T(1024)}, f32[1024]{0:T(1024)S(1)}, u32[]{:S(2)}) copy-start(f32[1024]{0:T(1024)S(1)} %broadcast_multiply_fusion.4) | copy-start | bytes 12292
  85.5 97.4 %copy-start.31 = (f32[1024]{0:T(1024)}, f32[1024]{0:T(1024)S(1)}, u32[]{:S(2)}) copy-start(f32[1024]{0:T(1024)S(1)} %add_rsqrt_fusion) | copy-start | bytes 12292
  85.5 19.2 %copy-start.46 = (bf16[1536,768]{1,0:T(8,128)(2,1)S(1)}, bf16[1536,768]{1,0:T(8,128)(2,1)}, u32[]{:S(2)}) copy-start(bf16[1536,768]{1,0:T(8,128)(2,1)} %param.30) | copy-start | bytes 7077892
  103.0 1.6 copy-start.54
  109.0 24.6 %copy-start.33 = (f32[768]{0:T(1024)S(1)}, f32[768]{0:T(1024)}, u32[]{:S(2)}) copy-start(f32[768]{0:T(1024)} %param.31) | copy-start | bytes 9220
  109.0 69.1 %all-reduce.10.cloned.1.call-start = ((), (), s32[]{:S(2)}) async-start(), calls=%async_computation.6 | async-start | bytes 6291456 | tf_op jit(solution)/shard_map/psum | solution.py:128
  124.4 13.8 %copy-start.53 = (s32[4]{0:T(128)}, s32[4]{0:T(128)S(1)}, u32[]{:S(2)}) copy-start(s32[4]{0:T(128)S(1)} %psum.93) | copy-start | bytes 52
  133.5 4.7 copy-start.47
  138.3 9.3 %copy-start.9 = (f32[1,1024,768]{2,1,0:T(8,128)}, f32[1,1024,768]{2,1,0:T(8,128)S(1)}, u32[]{:S(2)}) copy-start(f32[1,1024,768]{2,1,0:T(8,128)S(1)} %get-tuple-element.35) | copy-start | bytes 9437188
  147.5 1.6 copy-start.55
  153.6 124.5 %all-reduce.12.cloned.1.call-start = ((), (), s32[]{:S(2)}) async-start(), calls=%async_computation.7 | async-start | bytes 6291456 | tf_op jit(solution)/shard_map/psum | solution.py:179
  153.7 41.7 %copy-start.22 = (f32[6,512]{1,0:T(8,128)}, f32[6,512]{1,0:T(8,128)S(1)}, u32[]{:S(2)}) copy-start(f32[6,512]{1,0:T(8,128)S(1)} %log_add_fusion) | copy-start | bytes 36868
  178.1 13.7 %slice-start.6 = ((s8[12582912]{0:T(1024)(128)(4,1)}), s8[4194304]{0:T(1024)(128)(4,1)S(1)}, s32[]{:S(2)}) async-start(s8[12582912]{0:T(1024)(128)(4,1)} %bitcast.154), calls=%async_computation.18 | async-start | bytes 8388608
  182.9 7.3 copy-start.19
  182.9 8.9 %slice-start.7 = ((s8[12582912]{0:T(1024)(128)(4,1)}), s8[4194304]{0:T(1024)(128)(4,1)S(1)}, s32[]{:S(2)}) async-start(s8[12582912]{0:T(1024)(128)(4,1)} %bitcast.154), calls=%async_computation.19 | async-start | bytes 8388608
  182.9 8.9 %slice-start.8 = ((s8[12582912]{0:T(1024)(128)(4,1)}), s8[4194304]{0:T(1024)(128)(4,1)S(1)}, s32[]{:S(2)}) async-start(s8[12582912]{0:T(1024)(128)(4,1)} %bitcast.154), calls=%async_computation.20 | async-start | bytes 8388608
  190.2 1.7 copy-start.4
  191.8 10.6 %copy-start.15 = (bf16[1024,384]{0,1:T(8,128)(2,1)}, bf16[1024,384]{0,1:T(8,128)(2,1)S(1)}, u32[]{:S(2)}) copy-start(bf16[1024,384]{0,1:T(8,128)(2,1)S(1)} %convolution_convert_fusion) | copy-start | bytes 2359300
  191.9 10.6 %slice-start.3 = ((s8[12582912]{0:T(1024)(128)(4,1)}), s8[4194304]{0:T(1024)(128)(4,1)S(1)}, s32[]{:S(2)}) async-start(s8[12582912]{0:T(1024)(128)(4,1)} %bitcast.152), calls=%async_computation.15 | async-start | bytes 8388608
  191.9 10.6 %slice-start.4 = ((s8[12582912]{0:T(1024)(128)(4,1)}), s8[4194304]{0:T(1024)(128)(4,1)S(1)}, s32[]{:S(2)}) async-start(s8[12582912]{0:T(1024)(128)(4,1)} %bitcast.152), calls=%async_computation.16 | async-start | bytes 8388608
  195.4 7.1 slice-start.5
  208.8 6.5 copy-start.8
  215.3 2.7 copy-start.12
  218.0 1.2 copy-start.16
  218.1 1.7 copy-start.17
  239.5 1.8 copy-start.20
  241.3 5.7 copy-start.21
  247.0 154.5 %reduce-scatter.7.cloned.1.call-start = ((), (), s32[]{:S(2)}) async-start(), calls=%async_computation.9 | async-start | bytes 1253376 | tf_op jit(solution)/shard_map/reduce_scatter | solution.py:202
  252.1 290.6 %reduce-scatter.11.cloned.1.call-start = ((), (), s32[]{:S(2)}) async-start(), calls=%async_computation.11 | async-start | bytes 5013504 | tf_op jit(solution)/shard_map/reduce_scatter | solution.py:204
  260.5 424.5 %reduce-scatter.9.cloned.1.call-start = ((), (), s32[]{:S(2)}) async-start(), calls=%async_computation.10 | async-start | bytes 5013504 | tf_op jit(solution)/shard_map/reduce_scatter | solution.py:203
  269.4 1.4 copy-start.6
  269.4 1.4 copy-start.24
  269.4 1.4 copy-start.26
  269.4 1.4 copy-start.30
  269.4 1.4 copy-start.35
  269.4 1.4 copy-start.52
  269.4 553.7 %reduce-scatter.5.cloned.1.call-start = ((), (), s32[]{:S(2)}) async-start(), calls=%async_computation.8 | async-start | bytes 3760128 | tf_op jit(solution)/shard_map/reduce_scatter | solution.py:201
  276.3 1.7 copy-start.38
  278.1 3.4 copy-start.10
  281.4 541.7 %copy-start.1 = (bf16[768,1536]{1,0:T(8,128)(2,1)S(1)}, bf16[768,1536]{1,0:T(8,128)(2,1)}, u32[]{:S(2)}) copy-start(bf16[768,1536]{1,0:T(8,128)(2,1)} %param.28) | copy-start | bytes 7077892
  281.4 4.9 copy-start.36
  281.5 4.9 copy-start.37
  281.5 4.9 copy-start.41
  281.5 4.9 copy-start.42
  281.5 4.9 copy-start.43
  (9 other events, 7.1 us)
Sparse Core Ops, SparseCore 0:
  55.8 25.8 all-reduce.5
  109.1 24.3 all-reduce.7
  153.7 24.3 all-reduce.9
  247.1 24.3 all-reduce.11
  276.7 124.7 reduce-scatter.6
  407.1 135.4 reduce-scatter.10
  549.2 135.7 reduce-scatter.8
  690.8 132.3 reduce-scatter.4
where the time goes:
time: 837 us; the launch traced here: 830 us
  waiting for transfers between devices  517 us (62%)
  matrix products  123 us (15%)
  blocking collectives  92.5 us (11%)
  other arithmetic  65.7 us (8%)
  between operations  16.5 us (2%)
  local copies, waits for them, and re-layouts  14.7 us (2%)
    reduce_scatter x1, waiting for transfers between devices, local(): lax.psum_scatter(grad_up, 'dp', scatter_dimension=0, tiled=True)  142 us
    reduce_scatter x1, waiting for transfers between devices, local(): lax.psum_scatter(grad_down, 'dp', scatter_dimension=1, tiled=True)  141 us
    reduce_scatter x1, waiting for transfers between devices, local(): lax.psum_scatter(grad_qkv, 'dp', scatter_dimension=0, tiled=True)  138 us
    psum x1, blocking collectives, local(): lax.psum((grad_ln1_gain, grad_ln1_bias, qv_bias_grad, jnp.sum(mid_grad, a...  77.8 us
    reduce_scatter x1, waiting for transfers between devices, local(): lax.psum_scatter(grad_out, 'dp', scatter_dimension=1, tiled=True)  37.3 us
    psum x1, waiting for transfers between devices, local(): lax.psum(jnp.dot(mixed_heads, out_weight, preferred_element_type=jnp.floa...  26 us
    psum x1, waiting for transfers between devices, local(): lax.psum(jnp.einsum('tf,df->td', pre_grad_low, up_weight, preferred_eleme...  24.4 us
    dot_general x1, matrix products, local(): jnp.dot(ffn_in, up_weight, preferred_element_type=jnp.float32) + up_bias  17.6 us
  transfers between devices with their start and end apart: 8, of which 7 were waited for; matrix products, arithmetic and copies ran while one was open for 4% of the time, Pallas kernels for 0%

commit v1 on v0

--- a/solution.py
+++ b/solution.py
@@ -30,6 +30,71 @@
         - normed * jnp.mean(scaled * normed, axis=-1, keepdims=True)
     )
     return (inv_std * inner_part, jnp.sum(upstream * normed, axis=0), jnp.sum(upstream, axis=0))
+
+
+def pair_sum(value):
+    size = lax.axis_size("mp")
+    if size != 2:
+        return lax.psum(value, "mp")
+    return value + lax.ppermute(value, "mp", [(0, 1), (1, 0)])
+
+
+def xor_pairs(size, bit):
+    return [(index, index ^ bit) for index in range(size)]
+
+
+def axis_bits(size):
+    return [1 << place for place in range(size.bit_length() - 1)]
+
+
+def double_sum(value):
+    size = lax.axis_size("dp")
+    if size & (size - 1):
+        return lax.psum(value, "dp")
+    for bit in axis_bits(size):
+        value = value + lax.ppermute(value, "dp", xor_pairs(size, bit))
+    return value
+
+
+def section_orders(size):
+    bits = axis_bits(size)
+    if len(bits) == 4:
+        x_bit, y_bit, z_low, z_high = bits
+        return [
+            [x_bit, y_bit, z_low, z_high],
+            [y_bit, x_bit, z_low, z_high],
+            [z_low, x_bit, y_bit, z_high],
+        ]
+    third = max(1, len(bits) // 3)
+    return [bits[start:] + bits[:start] for start in (0, third, 2 * third)]
+
+
+def halve(section, order, size):
+    me = lax.axis_index("dp")
+    left = sorted(order, reverse=True)
+    rows, columns = section.shape
+    section = section.reshape((2,) * len(left) + (rows // size, columns))
+    for bit in order:
+        at = left.index(bit)
+        mine = (me // bit) % 2
+        send = lax.dynamic_index_in_dim(section, 1 - mine, at, keepdims=False)
+        keep = lax.dynamic_index_in_dim(section, mine, at, keepdims=False)
+        section = keep + lax.ppermute(send, "dp", xor_pairs(size, bit))
+        left.remove(bit)
+    return section
+
+
+def scatter_rows(grad):
+    size = lax.axis_size("dp")
+    if size & (size - 1):
+        return lax.psum_scatter(grad, "dp", scatter_dimension=0, tiled=True)
+    orders = section_orders(size)
+    width = grad.shape[1] // len(orders)
+    parts = [
+        halve(grad[:, place * width : (place + 1) * width], order, size)
+        for place, order in enumerate(orders)
+    ]
+    return jnp.concatenate(parts, axis=1)
 
 
 def local(
@@ -62,7 +127,7 @@
         + (timesteps >= NSTEPS // 4).astype(jnp.int32)
     )
     one_hot = buckets[:, None] == jnp.arange(NB, dtype=jnp.int32)[None, :]
-    bucket_counts = lax.psum(jnp.sum(one_hot.astype(jnp.int32), axis=0), "dp")
+    bucket_counts = double_sum(jnp.sum(one_hot.astype(jnp.int32), axis=0))
     floors = jnp.maximum(bucket_counts, 1).astype(jnp.float32)
     total_seqs = seq_count * lax.axis_size("dp")
     seq_weight = total_seqs / (NB * jnp.sum(jnp.where(one_hot, floors[None, :], 0.0), axis=1))
@@ -104,7 +169,7 @@
     mixed_heads = (
         jnp.concatenate(mixed_parts, axis=1).reshape(tok_rows, local_width).astype(jnp.bfloat16)
     )
-    attn_sum = lax.psum(jnp.dot(mixed_heads, out_weight, preferred_element_type=jnp.float32), "mp")
+    attn_sum = pair_sum(jnp.dot(mixed_heads, out_weight, preferred_element_type=jnp.float32))
     mid_state = residual + attn_sum + out_bias
     second_out, second_normed, second_inv = normalize(mid_state, ln2_gain, ln2_bias)
     ffn_in = second_out.astype(jnp.bfloat16)
@@ -113,20 +178,20 @@
         lambda inner_arg: jax.nn.gelu(inner_arg, approximate=False), preact
     )
     activated = gelu_value.astype(jnp.bfloat16)
-    ffn_sum = lax.psum(jnp.dot(activated, down_weight, preferred_element_type=jnp.float32), "mp")
+    ffn_sum = pair_sum(jnp.dot(activated, down_weight, preferred_element_type=jnp.float32))
     final_state = mid_state + ffn_sum + down_bias
     out_act = final_state.astype(jnp.bfloat16).reshape(seq_count, length, model_width)
     misfit = final_state.reshape(seq_count, length, model_width) - targets.astype(jnp.float32)
     out_grad = (misfit * seq_weight[:, None, None]).reshape(tok_rows, model_width)
     out_grad_low = out_grad.astype(jnp.bfloat16)
-    grad_down = jnp.einsum("tf,td->fd", activated, out_grad_low, preferred_element_type=jnp.float32)
+    grad_down = jnp.einsum("td,tf->df", out_grad_low, activated, preferred_element_type=jnp.float32)
     pre_grad = gelu_back(
         jnp.einsum("td,fd->tf", out_grad_low, down_weight, preferred_element_type=jnp.float32)
     )[0]
     pre_grad_low = pre_grad.astype(jnp.bfloat16)
     grad_up = jnp.einsum("td,tf->df", ffn_in, pre_grad_low, preferred_element_type=jnp.float32)
-    ffn_grad = lax.psum(
-        jnp.einsum("tf,df->td", pre_grad_low, up_weight, preferred_element_type=jnp.float32), "mp"
+    ffn_grad = pair_sum(
+        jnp.einsum("tf,df->td", pre_grad_low, up_weight, preferred_element_type=jnp.float32)
     )
     mid_back, grad_ln2_gain, grad_ln2_bias = norm_back(
         ffn_grad, second_normed, second_inv, ln2_gain
@@ -134,7 +199,7 @@
     mid_grad = out_grad + mid_back
     mid_grad_low = mid_grad.astype(jnp.bfloat16)
     grad_out = jnp.einsum(
-        "tk,td->kd", mixed_heads, mid_grad_low, preferred_element_type=jnp.float32
+        "td,tk->dk", mid_grad_low, mixed_heads, preferred_element_type=jnp.float32
     )
     mixed_grad = (
         jnp.einsum("td,kd->tk", mid_grad_low, out_weight, preferred_element_type=jnp.float32)
@@ -176,33 +241,40 @@
     qv_bias_grad = jnp.stack([jnp.sum(query_grad, axis=0), jnp.sum(value_flat, axis=0)])
     proj_grad = jnp.stack([query_grad, key_flat, value_flat], axis=1).astype(jnp.bfloat16)
     grad_qkv = jnp.einsum("td,tsk->dsk", attn_in, proj_grad, preferred_element_type=jnp.float32)
-    attn_grad = lax.psum(
-        jnp.einsum("tsk,dsk->td", proj_grad, qkv_weight, preferred_element_type=jnp.float32), "mp"
+    attn_grad = pair_sum(
+        jnp.einsum("tsk,dsk->td", proj_grad, qkv_weight, preferred_element_type=jnp.float32)
     )
     input_back, grad_ln1_gain, grad_ln1_bias = norm_back(
         attn_grad, first_normed, first_inv, ln1_gain
     )
     input_grad = (mid_grad + input_back).reshape(seq_count, length, model_width)
     grad_time = jnp.sum(input_grad, axis=1)
-    small_sums = lax.psum(
-        (
-            grad_ln1_gain,
-            grad_ln1_bias,
-            qv_bias_grad,
-            jnp.sum(mid_grad, axis=0),
-            grad_ln2_gain,
-            grad_ln2_bias,
-            jnp.sum(pre_grad, axis=0),
-            jnp.sum(out_grad, axis=0),
-        ),
-        "dp",
-    )
-    grad_qkv_part, grad_out_part, grad_up_part, grad_down_part = (
-        lax.psum_scatter(grad_qkv, "dp", scatter_dimension=0, tiled=True),
-        lax.psum_scatter(grad_out, "dp", scatter_dimension=1, tiled=True),
-        lax.psum_scatter(grad_up, "dp", scatter_dimension=0, tiled=True),
-        lax.psum_scatter(grad_down, "dp", scatter_dimension=1, tiled=True),
-    )
+    early = [
+        jnp.sum(mid_grad, axis=0),
+        grad_ln2_gain,
+        grad_ln2_bias,
+        jnp.sum(pre_grad, axis=0),
+        jnp.sum(out_grad, axis=0),
+    ]
+    late = [grad_ln1_gain, grad_ln1_bias, qv_bias_grad.reshape(-1)]
+    early_sum = double_sum(jnp.concatenate(early))
+    late_sum = double_sum(jnp.concatenate(late))
+    w = model_width
+    hidden = up_weight.shape[1]
+    small_sums = (
+        late_sum[:w],
+        late_sum[w : 2 * w],
+        late_sum[2 * w :].reshape(2, local_width),
+        early_sum[:w],
+        early_sum[w : 2 * w],
+        early_sum[2 * w : 3 * w],
+        early_sum[3 * w : 3 * w + hidden],
+        early_sum[3 * w + hidden :],
+    )
+    grad_qkv_part = scatter_rows(grad_qkv.reshape(w, 3 * local_width)).reshape(-1, 3, local_width)
+    grad_out_part = scatter_rows(grad_out).T
+    grad_up_part = scatter_rows(grad_up)
+    grad_down_part = scatter_rows(grad_down).T
     return (
         out_act,
         input_grad,

time: 837 us -> 450 us (0.54)
  waiting for transfers between devices: 517 us -> 136 us
  blocking collectives: 92.5 us -> 0 us
  starting transfers between devices: 0.54 us -> 83.2 us
  local copies, waits for them, and re-layouts: 14.7 us -> 43.3 us
  matrix products: 123 us -> 105 us
  between operations: 16.5 us -> 3.88 us
    reduce_scatter x4 -> x0, waiting for transfers between devices: 459 us -> none  [the longest x1 142 us: local(): lax.psum_scatter(grad_up, 'dp', scatter_dimension=0, tiled=True)]
    ppermute x0 -> x64, waiting for transfers between devices: none -> 136 us  [the longest x48 109 us: halve(): section = keep + lax.ppermute(send, 'dp', xor_pairs(size, bit))]
    psum x2 -> x0, blocking collectives: 92.5 us -> none  [the longest x1 77.8 us: local(): lax.psum((grad_ln1_gain, grad_ln1_bias, qv_bias_grad, jnp.sum(mid_grad, a...]
    ppermute x0 -> x64, starting transfers between devices: none -> 83.2 us  [the longest x48 65.1 us: halve(): section = keep + lax.ppermute(send, 'dp', xor_pairs(size, bit))]
    psum x4 -> x0, waiting for transfers between devices: 58.3 us -> none  [the longest x1 26 us: local(): lax.psum(jnp.dot(mixed_heads, out_weight, preferred_element_type=jnp.floa...]
    dynamic_slice x0 -> x21, local copies, waits for them, and re-layouts: none -> 9.73 us  [the longest x9 4.92 us: halve(): keep = lax.dynamic_index_in_dim(section, mine, at, keepdims=False)]
  transfers between devices with their start and end apart: 8 -> 64, of which waited for: 7 -> 40; matrix products, arithmetic and copies ran while one was open for 4% -> 10% of each run, Pallas kernels for 0% -> 0%
where the time goes in v1:
time: 450 us; the launch traced here: 443 us
  waiting for transfers between devices  136 us (30%)
  matrix products  105 us (23%)
  starting transfers between devices  83.2 us (18%)
  other arithmetic  71.5 us (16%)
  local copies, waits for them, and re-layouts  43.3 us (10%)
    ppermute x48, waiting for transfers between devices, halve(): section = keep + lax.ppermute(send, 'dp', xor_pairs(size, bit))  109 us
    ppermute x48, starting transfers between devices, halve(): section = keep + lax.ppermute(send, 'dp', xor_pairs(size, bit))  65.1 us
    ppermute x12, waiting for transfers between devices, double_sum(): value = value + lax.ppermute(value, 'dp', xor_pairs(size, bit))  21.4 us
    dot_general x1, matrix products, local(): jnp.dot(ffn_in, up_weight, preferred_element_type=jnp.float32) + up_bias  17.7 us
    ppermute x12, starting transfers between devices, double_sum(): value = value + lax.ppermute(value, 'dp', xor_pairs(size, bit))  17.1 us
    convert_element_type x2, other arithmetic, local(): score_grad = (attn_probs * (prob_grad - row_dot)).astype(jnp.bfloat16)  16.2 us
    dot_general x2, matrix products, local(): jnp.einsum('bqhe,bkhe->bhqk', grad_piece, values, preferred_element_type=...  13.5 us
    unnamed x146, local copies, waits for them, and re-layouts  12.9 us
  transfers between devices with their start and end apart: 64, of which 40 were waited for; matrix products, arithmetic and copies ran while one was open for 10% of the time, Pallas kernels for 0%

profile of v1, /device:TPU:0, one launch (start us, length us, event | category | flops | bytes accessed | tf_op | source)
XLA Modules:
  0.0 442.8 jit_solution(1514748159822732732)
XLA Ops:
  5.6 3.8 fusion.25
  13.2 6.4 %multiply_reduce_fusion.2 = (f32[6,512]{1,0:T(8,128)S(1)}, f32[6,512,1024]{2,1,0:T(8,128)}) fusion(bf16[1024,6,64]{0,2,1:T(8,128)(2,1)S(1)} %bitcast.370, bf16[1,1024,6,64]{1,3,2,0:T(8,128)(2,1)S(1)} %add_convert_fusion.3), kind=kOutput, calls=%fused_computation.12 | convolution fusion | flops 408941568 | bytes 13774848 | tf_op jit(solution)/shard_map/bqhe,bkhe->bhqk/dot_general | solution.py:147
  19.6 6.4 %multiply_reduce_fusion.3 = (f32[6,512]{1,0:T(8,128)S(1)}, f32[6,512,1024]{2,1,0:T(8,128)}) fusion(bf16[1024,6,64]{0,2,1:T(8,128)(2,1)S(1)} %bitcast.371, bf16[1,1024,6,64]{1,3,2,0:T(8,128)(2,1)S(1)} %add_convert_fusion.3), kind=kOutput, calls=%fused_computation.13 | convolution fusion | flops 408941568 | bytes 13774848 | tf_op jit(solution)/shard_map/bqhe,bkhe->bhqk/dot_general | solution.py:147
  27.9 7.8 %fusion.1 = f32[6,512]{1,0:T(8,128)S(1)} fusion(f32[6,512,1024]{2,1,0:T(8,128)} %get-tuple-element.125, f32[6,512]{1,0:T(8,128)S(1)} %get-tuple-element.124), kind=kLoop, calls=%fused_computation.11 | loop fusion | flops 9434112 | bytes 12607488 | tf_op jit(solution)/shard_map/reduce_sum | solution.py:158
  35.7 3.6 fusion.52
  39.4 2.8 fusion
  42.2 3.6 fusion.51
  47.6 5.3 %collective-permute-done = f32[1024,768]{1,0:T(8,128)S(1)} collective-permute-done((f32[1024,768]{1,0:T(8,128)S(1)}, f32[1024,768]{1,0:T(8,128)S(1)}, u32[]{:S(2)}, u32[]{:S(2)}) %collective-permute-start) | collective-permute-done | bytes 3145760 | tf_op jit(solution)/shard_map/ppermute | solution.py:39
  54.4 17.7 %multiply_convert_fusion.2 = (bf16[1024,1536]{1,0:T(8,128)(2,1)S(1)}, f32[1024,1536]{1,0:T(8,128)}, f32[1024,1536]{1,0:T(8,128)}) fusion(f32[1536]{0:T(1024)S(1)} %copy-done.56, bf16[768,1536]{1,0:T(8,128)(2,1)S(1)} %copy-done, f32[1024,768]{1,0:T(8,128)S(1)} %get-tuple-element.73, f32[768]{0:T(1024)S(1)} %copy-done.57, f32[768]{0:T(1024)S(1)} %copy-done.40, ...), kind=kOutput, calls=%fused_computation.23 | convolution fusion | flops 2523660288 | bytes 21254144 | tf_op jit(solution)/shard_map/dot_general | solution.py:176
  72.2 4.2 fusion.88
  77.5 2.7 collective-permute-start.2
  88.9 3.0 collective-permute-start.5
  95.3 5.7 %fusion.54 = (f32[768]{0:T(1024)}, f32[1024,768]{1,0:T(8,128)S(1)}) fusion(f32[]{:T(128)S(6)} %div.121, bf16[1,1024,768]{2,1,0:T(8,128)(2,1)} %param.18, f32[768]{0:T(1024)S(1)} %copy-done.51, f32[1024,768]{1,0:T(8,128)} %copy-done.3, f32[1024,768]{1,0:T(8,128)} %fusion.88, f32[1024,768]{1,0:T(8,128)} %collective-permute-done.1), kind=kLoop, calls=%fused_computation.103 | loop fusion | flops 5504256 | bytes 14161924 | tf_op jit(solution)/shard_map/reduce_sum | solution.py:257
  102.8 2.7 fusion.89
  107.2 8.4 %fusion.72 = (f32[1536]{0:T(1024)}, bf16[1024,1536]{1,0:T(8,128)(2,1)S(1)}) fusion(f32[1024,1536]{1,0:T(8,128)} %get-tuple-element.71, f32[1024,1536]{1,0:T(8,128)} %get-tuple-element.128, f32[1536]{0:T(1024)S(1)} %copy-done.56, bf16[1024,768]{1,0:T(8,128)(2,1)S(1)} %bitcast_convert_fusion, bf16[1536,768]{1,0:T(8,128)(2,1)S(1)} %copy-done.54), kind=kOutput, calls=%fused_computation.273 | convolution fusion | flops 2441083392 | bytes 19673088 | tf_op jit(solution)/shard_map/td,fd->tf/dot_general | solution.py:189
  117.2 3.0 fusion.34
  128.5 2.6 fusion.36
  131.2 11.3 %collective-permute-done.48 = f32[2,2,2,48,512]{4,3,1,0,2:T(8,128)S(1)} collective-permute-done((f32[2,2,2,48,512]{4,3,1,0,2:T(8,128)S(1)}, f32[2,2,2,48,512]{4,3,1,0,2:T(8,128)S(1)}, u32[]{:S(2)}, u32[]{:S(2)}) %collective-permute-start.48) | collective-permute-done | bytes 786464 | tf_op jit(solution)/shard_map/ppermute | solution.py:82
  145.2 11.1 %collective-permute-done.56 = f32[2,2,2,48,512]{4,3,1,0,2:T(8,128)S(1)} collective-permute-done((f32[2,2,2,48,512]{4,3,1,0,2:T(8,128)S(1)}, f32[2,2,2,48,512]{4,3,1,0,2:T(8,128)S(1)}, u32[]{:S(2)}, u32[]{:S(2)}) %collective-permute-start.56) | collective-permute-done | bytes 786464 | tf_op jit(solution)/shard_map/ppermute | solution.py:82
  164.2 6.6 %collective-permute-done.49 = f32[2,2,48,512]{3,2,1,0:T(8,128)S(1)} collective-permute-done((f32[2,2,48,512]{3,2,1,0:T(8,128)S(1)}, f32[2,2,48,512]{3,2,1,0:T(8,128)S(1)}, u32[]{:S(2)}, u32[]{:S(2)}) %collective-permute-start.49) | collective-permute-done | bytes 393248 | tf_op jit(solution)/shard_map/ppermute | solution.py:82
  172.4 6.7 %collective-permute-done.45 = f32[2,2,48,512]{3,2,1,0:T(8,128)S(1)} collective-permute-done((f32[2,2,48,512]{3,2,1,0:T(8,128)S(1)}, f32[2,2,48,512]{3,2,1,0:T(8,128)S(1)}, u32[]{:S(2)}, u32[]{:S(2)}) %collective-permute-start.45) | collective-permute-done | bytes 393248 | tf_op jit(solution)/shard_map/ppermute | solution.py:82
  180.9 6.5 %collective-permute-done.57 = f32[2,2,48,512]{3,2,1,0:T(8,128)S(1)} collective-permute-done((f32[2,2,48,512]{3,2,1,0:T(8,128)S(1)}, f32[2,2,48,512]{3,2,1,0:T(8,128)S(1)}, u32[]{:S(2)}, u32[]{:S(2)}) %collective-permute-start.57) | collective-permute-done | bytes 393248 | tf_op jit(solution)/shard_map/ppermute | solution.py:82
  189.1 2.6 collective-permute-done.61
  197.4 5.2 %collective-permute-done.46 = f32[2,48,512]{2,1,0:T(8,128)S(1)} collective-permute-done((f32[2,48,512]{2,1,0:T(8,128)S(1)}, f32[2,48,512]{2,1,0:T(8,128)S(1)}, u32[]{:S(2)}, u32[]{:S(2)}) %collective-permute-start.46) | collective-permute-done | bytes 196640 | tf_op jit(solution)/shard_map/ppermute | solution.py:82
  202.7 3.1 collective-permute-done.58
  211.7 3.1 collective-permute-start.63
  214.8 4.8 %collective-permute-done.51 = f32[48,512]{1,0:T(8,128)S(1)} collective-permute-done((f32[48,512]{1,0:T(8,128)S(1)}, f32[48,512]{1,0:T(8,128)S(1)}, u32[]{:S(2)}, u32[]{:S(2)}) %collective-permute-start.51) | collective-permute-done | bytes 98336 | tf_op jit(solution)/shard_map/ppermute | solution.py:82
  219.6 3.1 collective-permute-done.47
  223.8 2.1 collective-permute-done.63
  229.8 2.4 multiply_reduce_fusion.4
  232.2 3.3 fusion.73
  239.7 3.5 fusion.4
  243.2 7.0 %multiply_reduce_fusion = (f32[6,512]{1,0:T(8,128)}, f32[6,512,1024]{2,1,0:T(8,128)}) fusion(f32[6,512,1024]{2,1,0:T(8,128)S(1)} %bitcast.369, f32[6,512]{1,0:T(8,128)S(1)} %log_add_fusion, bf16[1024,6,64]{0,2,1:T(8,128)(2,1)S(1)} %add_convert_fusion.4, bf16[1,1024,6,64]{1,3,2,0:T(8,128)(2,1)S(1)} %bitcast.377), kind=kOutput, calls=%fused_computation.1 | convolution fusion | flops 415233024 | bytes 26374144 | tf_op jit(solution)/shard_map/bqhe,bkhe->bhqk/dot_general | solution.py:216
  250.3 6.4 %multiply_reduce_fusion.1 = (f32[6,512]{1,0:T(8,128)S(1)}, f32[6,512,1024]{2,1,0:T(8,128)}) fusion(f32[6,512,1024]{2,1,0:T(8,128)S(1)} %bitcast.367, f32[6,512]{1,0:T(8,128)S(1)} %log_add_fusion.1, bf16[1024,6,64]{0,2,1:T(8,128)(2,1)S(1)} %add_convert_fusion.4, bf16[1,1024,6,64]{1,3,2,0:T(8,128)(2,1)S(1)} %bitcast.378), kind=kOutput, calls=%fused_computation.4 | convolution fusion | flops 415233024 | bytes 26374144 | tf_op jit(solution)/shard_map/bqhe,bkhe->bhqk/dot_general | solution.py:216
  256.7 6.5 %multiply_convert_fusion.1 = bf16[6,512,1024]{2,1,0:T(8,128)(2,1)S(1)} fusion(f32[6,512,1024]{2,1,0:T(8,128)} %get-tuple-element.130, f32[6,512,1024]{2,1,0:T(8,128)S(1)} %bitcast.367, f32[6,512]{1,0:T(8,128)S(1)} %get-tuple-element.129, f32[6,512]{1,0:T(8,128)S(1)} %log_add_fusion.1), kind=kLoop, calls=%fused_computation.3 | loop fusion | flops 15728640 | bytes 31481856 | tf_op jit(solution)/shard_map/convert_element_type | solution.py:220
  263.3 2.7 fusion.84
  267.7 3.7 bitcast_convert_fusion.1
  271.3 2.3 copy.63
  273.6 9.7 %multiply_convert_fusion = bf16[6,512,1024]{2,1,0:T(8,128)(2,1)S(1)} fusion(f32[6,512,1024]{2,1,0:T(8,128)} %get-tuple-element.132, f32[6,512,1024]{2,1,0:T(8,128)} %get-tuple-element.125, f32[6,512]{1,0:T(8,128)} %get-tuple-element.131, f32[6,512]{1,0:T(8,128)} %copy-done.33), kind=kLoop, calls=%fused_computation | loop fusion | flops 15728640 | bytes 31481856 | tf_op jit(solution)/shard_map/convert_element_type | solution.py:220
  283.3 3.4 fusion.83
  294.8 5.1 %convolution_bitcast_fusion = f32[1024,768]{1,0:T(8,128)} fusion(bf16[768,3,384]{2,0,1:T(8,128)(2,1)S(1)} %copy-done.55, bf16[1024,1,384]{2,0,1:T(8,128)(2,1)S(1)} %copy-done.23, bf16[1024,1,384]{2,0,1:T(8,128)(2,1)S(1)} %copy.62, bf16[1024,1,384]{2,0,1:T(8,128)(2,1)} %copy-done.24), kind=kOutput, calls=%fused_computation.66 | convolution fusion | flops 1814298624 | bytes 7274496 | tf_op jit(solution)/shard_map/tsk,dsk->td/dot_general | solution.py:245
  314.5 4.6 %copy.64 = bf16[3,384,1024]{2,1,0:T(8,128)(2,1)} copy(bf16[3,384,1024]{1,2,0:T(8,128)(2,1)} %fusion.53) | data formatting | bytes 4718592 | tf_op jit(solution)/shard_map/td,tsk->dsk/dot_general | solution.py:243
  319.1 4.4 fusion.28
  339.7 6.7 %collective-permute-done.39 = f32[4608]{0:T(1024)S(1)} collective-permute-done((f32[4608]{0:T(1024)S(1)}, f32[4608]{0:T(1024)S(1)}, u32[]{:S(2)}, u32[]{:S(2)}) %collective-permute-start.39) | collective-permute-done | bytes 18464 | tf_op jit(solution)/shard_map/ppermute | solution.py:55
  354.3 7.2 %collective-permute-done.33 = f32[2,2,48,128]{3,2,1,0:T(8,128)S(1)} collective-permute-done((f32[2,2,48,128]{3,2,1,0:T(8,128)S(1)}, f32[2,2,48,128]{3,2,1,0:T(8,128)S(1)}, u32[]{:S(2)}, u32[]{:S(2)}) %collective-permute-start.33) | collective-permute-done | bytes 98336 | tf_op jit(solution)/shard_map/ppermute | solution.py:82
  361.5 2.2 collective-permute-start.29
  363.7 2.6 collective-permute-done.29
  366.8 4.1 collective-permute-done.25
  371.4 3.6 collective-permute-done.34
  375.0 2.5 collective-permute-start.30
  377.5 2.3 collective-permute-done.30
  381.7 2.2 collective-permute-done.26
  383.9 2.7 collective-permute-start.35
  388.6 2.7 collective-permute-start.31
  393.4 2.7 collective-permute-start.27
  401.8 3.9 collective-permute-done.21
  406.3 2.5 collective-permute-done.17
  411.1 3.0 collective-permute-start.23
  414.2 2.9 collective-permute-start.19
  419.6 3.8 collective-permute-done.15
  423.4 2.2 multiply_reduce_fusion.5
  429.9 3.2 collective-permute-done.9
  433.1 3.7 collective-permute-done.10
  437.8 2.5 fusion.74
  (416 shorter events, 148.9 us)
Async XLA Ops:
  47.0 5.8 %collective-permute-start = (f32[1024,768]{1,0:T(8,128)S(1)}, f32[1024,768]{1,0:T(8,128)S(1)}, u32[]{:S(2)}, u32[]{:S(2)}) collective-permute-start(f32[1024,768]{1,0:T(8,128)S(1)} %fusion.87), channel_id=1, source_target_pairs={{0,1},{1,0},{2,3},{3,2},{4,5},{5,4},{6,7},{7,6},{8,9},{9,8},{10,11... | collective-permute-start | bytes 9437192 | tf_op jit(solution)/shard_map/ppermute | solution.py:39
  76.4 18.8 %collective-permute-start.1 = (f32[1024,768]{1,0:T(8,128)}, f32[1024,768]{1,0:T(8,128)}, u32[]{:S(2)}, u32[]{:S(2)}) collective-permute-start(f32[1024,768]{1,0:T(8,128)} %fusion.88), channel_id=1, source_target_pairs={{0,1},{1,0},{2,3},{3,2},{4,5},{5,4},{6,7},{7,6},{8,9},{9,8},{10,11... | collective-permute-start | bytes 9437192 | tf_op jit(solution)/shard_map/ppermute | solution.py:39
  77.5 4.2 collective-permute-start.2
  81.7 3.6 collective-permute-start.3
  85.3 3.6 collective-permute-start.4
  88.9 4.6 %collective-permute-start.5 = (s32[4]{0:T(128)S(1)}, s32[4]{0:T(128)S(1)}, u32[]{:S(2)}, u32[]{:S(2)}) collective-permute-start(s32[4]{0:T(128)S(1)} %add.572), channel_id=1, source_target_pairs={{0,16},{2,18},{4,20},{6,22},{8,24},{10,26},{12,28},{14,30},{16,0},... | collective-permute-start | bytes 56 | tf_op jit(solution)/shard_map/ppermute | solution.py:55
  121.9 20.5 %collective-permute-start.48 = (f32[2,2,2,48,512]{4,3,1,0,2:T(8,128)S(1)}, f32[2,2,2,48,512]{4,3,1,0,2:T(8,128)S(1)}, u32[]{:S(2)}, u32[]{:S(2)}) collective-permute-start(f32[2,2,2,48,512]{4,3,1,0,2:T(8,128)S(1)} %bitcast.404), channel_id=1, source_target_pairs={{0,8},{2,10},{4,12},{6,14},{8,0},{10,2},{12,4},{14,6},{16,24},{18,... | collective-permute-start | bytes 2359304 | tf_op jit(solution)/shard_map/ppermute | solution.py:82
  124.5 20.5 %collective-permute-start.44 = (f32[2,2,2,48,512]{4,3,1,0,2:T(8,128)S(1)}, f32[2,2,2,48,512]{4,3,1,0,2:T(8,128)S(1)}, u32[]{:S(2)}, u32[]{:S(2)}) collective-permute-start(f32[2,2,2,48,512]{4,3,1,0,2:T(8,128)S(1)} %bitcast.405), channel_id=1, source_target_pairs={{0,4},{2,6},{4,0},{6,2},{8,12},{10,14},{12,8},{14,10},{16,20},{18,... | collective-permute-start | bytes 2359304 | tf_op jit(solution)/shard_map/ppermute | solution.py:82
  126.1 30.3 %collective-permute-start.56 = (f32[2,2,2,48,512]{4,3,1,0,2:T(8,128)S(1)}, f32[2,2,2,48,512]{4,3,1,0,2:T(8,128)S(1)}, u32[]{:S(2)}, u32[]{:S(2)}) collective-permute-start(f32[2,2,2,48,512]{4,3,1,0,2:T(8,128)S(1)} %bitcast.403), channel_id=1, source_target_pairs={{0,4},{2,6},{4,0},{6,2},{8,12},{10,14},{12,8},{14,10},{16,20},{18,... | collective-permute-start | bytes 2359304 | tf_op jit(solution)/shard_map/ppermute | solution.py:82
  126.6 31.4 %collective-permute-start.60 = (f32[2,2,2,48,512]{4,3,1,0,2:T(8,128)S(1)}, f32[2,2,2,48,512]{4,3,1,0,2:T(8,128)S(1)}, u32[]{:S(2)}, u32[]{:S(2)}) collective-permute-start(f32[2,2,2,48,512]{4,3,1,0,2:T(8,128)S(1)} %bitcast.402), channel_id=1, source_target_pairs={{0,8},{2,10},{4,12},{6,14},{8,0},{10,2},{12,4},{14,6},{16,24},{18,... | collective-permute-start | bytes 2359304 | tf_op jit(solution)/shard_map/ppermute | solution.py:82
  126.7 32.1 %collective-permute-start.40 = (f32[2,2,2,48,512]{4,3,1,0,2:T(8,128)S(1)}, f32[2,2,2,48,512]{4,3,1,0,2:T(8,128)S(1)}, u32[]{:S(2)}, u32[]{:S(2)}) collective-permute-start(f32[2,2,2,48,512]{4,3,1,0,2:T(8,128)S(1)} %bitcast.401), channel_id=1, source_target_pairs={{0,2},{2,0},{4,6},{6,4},{8,10},{10,8},{12,14},{14,12},{16,18},{18,... | collective-permute-start | bytes 2359304 | tf_op jit(solution)/shard_map/ppermute | solution.py:82
  142.5 19.8 %collective-permute-start.52 = (f32[2,2,2,48,512]{4,3,1,0,2:T(8,128)S(1)}, f32[2,2,2,48,512]{4,3,1,0,2:T(8,128)S(1)}, u32[]{:S(2)}, u32[]{:S(2)}) collective-permute-start(f32[2,2,2,48,512]{4,3,1,0,2:T(8,128)S(1)} %bitcast.400), channel_id=1, source_target_pairs={{0,2},{2,0},{4,6},{6,4},{8,10},{10,8},{12,14},{14,12},{16,18},{18,... | collective-permute-start | bytes 2359304 | tf_op jit(solution)/shard_map/ppermute | solution.py:82
  145.0 84.7 %collective-permute-start.6 = (f32[1024,768]{1,0:T(8,128)S(1)}, f32[1024,768]{1,0:T(8,128)S(1)}, u32[]{:S(2)}, u32[]{:S(2)}) collective-permute-start(f32[1024,768]{1,0:T(8,128)S(1)} %fusion.36), channel_id=1, source_target_pairs={{0,1},{1,0},{2,3},{3,2},{4,5},{5,4},{6,7},{7,6},{8,9},{9,8},{10,11... | collective-permute-start | bytes 9437192 | tf_op jit(solution)/shard_map/ppermute | solution.py:39
  156.4 14.4 %collective-permute-start.49 = (f32[2,2,48,512]{3,2,1,0:T(8,128)S(1)}, f32[2,2,48,512]{3,2,1,0:T(8,128)S(1)}, u32[]{:S(2)}, u32[]{:S(2)}) collective-permute-start(f32[2,2,48,512]{3,2,1,0:T(8,128)S(1)} %dynamic-slice_bitcast_fusion.3), channel_id=1, source_target_pairs={{0,2},{2,0},{4,6},{6,4},{8,10},{10,8},{12,14},{14,12},{16,18},{18,... | collective-permute-start | bytes 1179656 | tf_op jit(solution)/shard_map/ppermute | solution.py:82
  158.0 21.1 %collective-permute-start.45 = (f32[2,2,48,512]{3,2,1,0:T(8,128)S(1)}, f32[2,2,48,512]{3,2,1,0:T(8,128)S(1)}, u32[]{:S(2)}, u32[]{:S(2)}) collective-permute-start(f32[2,2,48,512]{3,2,1,0:T(8,128)S(1)} %dynamic-slice_bitcast_fusion.4), channel_id=1, source_target_pairs={{0,2},{2,0},{4,6},{6,4},{8,10},{10,8},{12,14},{14,12},{16,18},{18,... | collective-permute-start | bytes 1179656 | tf_op jit(solution)/shard_map/ppermute | solution.py:82
  158.8 28.6 %collective-permute-start.57 = (f32[2,2,48,512]{3,2,1,0:T(8,128)S(1)}, f32[2,2,48,512]{3,2,1,0:T(8,128)S(1)}, u32[]{:S(2)}, u32[]{:S(2)}) collective-permute-start(f32[2,2,48,512]{3,2,1,0:T(8,128)S(1)} %dynamic-slice_bitcast_fusion.1), channel_id=1, source_target_pairs={{0,2},{2,0},{4,6},{6,4},{8,10},{10,8},{12,14},{14,12},{16,18},{18,... | collective-permute-start | bytes 1179656 | tf_op jit(solution)/shard_map/ppermute | solution.py:82
  162.3 29.3 %collective-permute-start.61 = (f32[2,2,48,512]{3,2,1,0:T(8,128)S(1)}, f32[2,2,48,512]{3,2,1,0:T(8,128)S(1)}, u32[]{:S(2)}, u32[]{:S(2)}) collective-permute-start(f32[2,2,48,512]{3,2,1,0:T(8,128)S(1)} %dynamic-slice_bitcast_fusion), channel_id=1, source_target_pairs={{0,2},{2,0},{4,6},{6,4},{8,10},{10,8},{12,14},{14,12},{16,18},{18,... | collective-permute-start | bytes 1179656 | tf_op jit(solution)/shard_map/ppermute | solution.py:82
  170.7 22.7 %collective-permute-start.41 = (f32[2,2,48,512]{3,2,1,0:T(8,128)S(1)}, f32[2,2,48,512]{3,2,1,0:T(8,128)S(1)}, u32[]{:S(2)}, u32[]{:S(2)}) collective-permute-start(f32[2,2,48,512]{3,2,1,0:T(8,128)S(1)} %dynamic-slice_bitcast_fusion.5), channel_id=1, source_target_pairs={{0,4},{2,6},{4,0},{6,2},{8,12},{10,14},{12,8},{14,10},{16,20},{18,... | collective-permute-start | bytes 1179656 | tf_op jit(solution)/shard_map/ppermute | solution.py:82
  179.2 14.8 %collective-permute-start.53 = (f32[2,2,48,512]{3,2,1,0:T(8,128)S(1)}, f32[2,2,48,512]{3,2,1,0:T(8,128)S(1)}, u32[]{:S(2)}, u32[]{:S(2)}) collective-permute-start(f32[2,2,48,512]{3,2,1,0:T(8,128)S(1)} %dynamic-slice_bitcast_fusion.2), channel_id=1, source_target_pairs={{0,4},{2,6},{4,0},{6,2},{8,12},{10,14},{12,8},{14,10},{16,20},{18,... | collective-permute-start | bytes 1179656 | tf_op jit(solution)/shard_map/ppermute | solution.py:82
  187.4 8.3 %collective-permute-start.50 = (f32[2,48,512]{2,1,0:T(8,128)S(1)}, f32[2,48,512]{2,1,0:T(8,128)S(1)}, u32[]{:S(2)}, u32[]{:S(2)}) collective-permute-start(f32[2,48,512]{2,1,0:T(8,128)S(1)} %dynamic-slice_bitcast_fusion.12), channel_id=1, source_target_pairs={{0,4},{2,6},{4,0},{6,2},{8,12},{10,14},{12,8},{14,10},{16,20},{18,... | collective-permute-start | bytes 589832 | tf_op jit(solution)/shard_map/ppermute | solution.py:82
  191.6 11.0 %collective-permute-start.46 = (f32[2,48,512]{2,1,0:T(8,128)S(1)}, f32[2,48,512]{2,1,0:T(8,128)S(1)}, u32[]{:S(2)}, u32[]{:S(2)}) collective-permute-start(f32[2,48,512]{2,1,0:T(8,128)S(1)} %dynamic-slice_bitcast_fusion.13), channel_id=1, source_target_pairs={{0,8},{2,10},{4,12},{6,14},{8,0},{10,2},{12,4},{14,6},{16,24},{18,... | collective-permute-start | bytes 589832 | tf_op jit(solution)/shard_map/ppermute | solution.py:82
  193.4 12.4 %collective-permute-start.58 = (f32[2,48,512]{2,1,0:T(8,128)S(1)}, f32[2,48,512]{2,1,0:T(8,128)S(1)}, u32[]{:S(2)}, u32[]{:S(2)}) collective-permute-start(f32[2,48,512]{2,1,0:T(8,128)S(1)} %dynamic-slice_bitcast_fusion.10), channel_id=1, source_target_pairs={{0,8},{2,10},{4,12},{6,14},{8,0},{10,2},{12,4},{14,6},{16,24},{18,... | collective-permute-start | bytes 589832 | tf_op jit(solution)/shard_map/ppermute | solution.py:82
  194.0 13.0 %collective-permute-start.62 = (f32[2,48,512]{2,1,0:T(8,128)S(1)}, f32[2,48,512]{2,1,0:T(8,128)S(1)}, u32[]{:S(2)}, u32[]{:S(2)}) collective-permute-start(f32[2,48,512]{2,1,0:T(8,128)S(1)} %dynamic-slice_bitcast_fusion.9), channel_id=1, source_target_pairs={{0,4},{2,6},{4,0},{6,2},{8,12},{10,14},{12,8},{14,10},{16,20},{18,... | collective-permute-start | bytes 589832 | tf_op jit(solution)/shard_map/ppermute | solution.py:82
  195.7 13.2 %collective-permute-start.42 = (f32[2,48,512]{2,1,0:T(8,128)S(1)}, f32[2,48,512]{2,1,0:T(8,128)S(1)}, u32[]{:S(2)}, u32[]{:S(2)}) collective-permute-start(f32[2,48,512]{2,1,0:T(8,128)S(1)} %dynamic-slice_bitcast_fusion.14), channel_id=1, source_target_pairs={{0,8},{2,10},{4,12},{6,14},{8,0},{10,2},{12,4},{14,6},{16,24},{18,... | collective-permute-start | bytes 589832 | tf_op jit(solution)/shard_map/ppermute | solution.py:82
  202.6 9.0 %collective-permute-start.54 = (f32[2,48,512]{2,1,0:T(8,128)S(1)}, f32[2,48,512]{2,1,0:T(8,128)S(1)}, u32[]{:S(2)}, u32[]{:S(2)}) collective-permute-start(f32[2,48,512]{2,1,0:T(8,128)S(1)} %dynamic-slice_bitcast_fusion.11), channel_id=1, source_target_pairs={{0,8},{2,10},{4,12},{6,14},{8,0},{10,2},{12,4},{14,6},{16,24},{18,... | collective-permute-start | bytes 589832 | tf_op jit(solution)/shard_map/ppermute | solution.py:82
  205.8 13.8 %collective-permute-start.51 = (f32[48,512]{1,0:T(8,128)S(1)}, f32[48,512]{1,0:T(8,128)S(1)}, u32[]{:S(2)}, u32[]{:S(2)}) collective-permute-start(f32[48,512]{1,0:T(8,128)S(1)} %dynamic-slice_bitcast_fusion.21), channel_id=1, source_target_pairs={{0,16},{2,18},{4,20},{6,22},{8,24},{10,26},{12,28},{14,30},{16,0},... | collective-permute-start | bytes 294920 | tf_op jit(solution)/shard_map/ppermute | solution.py:82
  206.9 15.8 %collective-permute-start.47 = (f32[48,512]{1,0:T(8,128)S(1)}, f32[48,512]{1,0:T(8,128)S(1)}, u32[]{:S(2)}, u32[]{:S(2)}) collective-permute-start(f32[48,512]{1,0:T(8,128)S(1)} %dynamic-slice_bitcast_fusion.22), channel_id=1, source_target_pairs={{0,16},{2,18},{4,20},{6,22},{8,24},{10,26},{12,28},{14,30},{16,0},... | collective-permute-start | bytes 294920 | tf_op jit(solution)/shard_map/ppermute | solution.py:82
  208.9 14.9 %collective-permute-start.59 = (f32[48,512]{1,0:T(8,128)S(1)}, f32[48,512]{1,0:T(8,128)S(1)}, u32[]{:S(2)}, u32[]{:S(2)}) collective-permute-start(f32[48,512]{1,0:T(8,128)S(1)} %dynamic-slice_bitcast_fusion.19), channel_id=1, source_target_pairs={{0,16},{2,18},{4,20},{6,22},{8,24},{10,26},{12,28},{14,30},{16,0},... | collective-permute-start | bytes 294920 | tf_op jit(solution)/shard_map/ppermute | solution.py:82
  211.7 14.3 %collective-permute-start.63 = (f32[48,512]{1,0:T(8,128)S(1)}, f32[48,512]{1,0:T(8,128)S(1)}, u32[]{:S(2)}, u32[]{:S(2)}) collective-permute-start(f32[48,512]{1,0:T(8,128)S(1)} %dynamic-slice_bitcast_fusion.18), channel_id=1, source_target_pairs={{0,16},{2,18},{4,20},{6,22},{8,24},{10,26},{12,28},{14,30},{16,0},... | collective-permute-start | bytes 294920 | tf_op jit(solution)/shard_map/ppermute | solution.py:82
  219.6 7.4 %collective-permute-start.43 = (f32[48,512]{1,0:T(8,128)S(1)}, f32[48,512]{1,0:T(8,128)S(1)}, u32[]{:S(2)}, u32[]{:S(2)}) collective-permute-start(f32[48,512]{1,0:T(8,128)S(1)} %dynamic-slice_bitcast_fusion.23), channel_id=1, source_target_pairs={{0,16},{2,18},{4,20},{6,22},{8,24},{10,26},{12,28},{14,30},{16,0},... | collective-permute-start | bytes 294920 | tf_op jit(solution)/shard_map/ppermute | solution.py:82
  222.8 5.5 %collective-permute-start.55 = (f32[48,512]{1,0:T(8,128)S(1)}, f32[48,512]{1,0:T(8,128)S(1)}, u32[]{:S(2)}, u32[]{:S(2)}) collective-permute-start(f32[48,512]{1,0:T(8,128)S(1)} %dynamic-slice_bitcast_fusion.20), channel_id=1, source_target_pairs={{0,16},{2,18},{4,20},{6,22},{8,24},{10,26},{12,28},{14,30},{16,0},... | collective-permute-start | bytes 294920 | tf_op jit(solution)/shard_map/ppermute | solution.py:82
  306.5 18.1 %collective-permute-start.36 = (f32[4608]{0:T(1024)}, f32[4608]{0:T(1024)}, u32[]{:S(2)}, u32[]{:S(2)}) collective-permute-start(f32[4608]{0:T(1024)} %constant_dynamic-update-slice_fusion), channel_id=1, source_target_pairs={{0,2},{2,0},{4,6},{6,4},{8,10},{10,8},{12,14},{14,12},{16,18},{18,... | collective-permute-start | bytes 55304 | tf_op jit(solution)/shard_map/ppermute | solution.py:55
  310.2 38.9 %collective-permute-start.32 = (f32[2,2,2,48,128]{4,3,1,0,2:T(8,128)}, f32[2,2,2,48,128]{4,3,1,0,2:T(8,128)}, u32[]{:S(2)}, u32[]{:S(2)}) collective-permute-start(f32[2,2,2,48,128]{4,3,1,0,2:T(8,128)} %bitcast.361), channel_id=1, source_target_pairs={{0,8},{2,10},{4,12},{6,14},{8,0},{10,2},{12,4},{14,6},{16,24},{18,... | collective-permute-start | bytes 589832 | tf_op jit(solution)/shard_map/ppermute | solution.py:82
  311.6 40.0 %collective-permute-start.28 = (f32[2,2,2,48,128]{4,3,1,0,2:T(8,128)}, f32[2,2,2,48,128]{4,3,1,0,2:T(8,128)}, u32[]{:S(2)}, u32[]{:S(2)}) collective-permute-start(f32[2,2,2,48,128]{4,3,1,0,2:T(8,128)} %bitcast.362), channel_id=1, source_target_pairs={{0,4},{2,6},{4,0},{6,2},{8,12},{10,14},{12,8},{14,10},{16,20},{18,... | collective-permute-start | bytes 589832 | tf_op jit(solution)/shard_map/ppermute | solution.py:82
  313.2 39.6 %collective-permute-start.24 = (f32[2,2,2,48,128]{4,3,1,0,2:T(8,128)}, f32[2,2,2,48,128]{4,3,1,0,2:T(8,128)}, u32[]{:S(2)}, u32[]{:S(2)}) collective-permute-start(f32[2,2,2,48,128]{4,3,1,0,2:T(8,128)} %bitcast.363), channel_id=1, source_target_pairs={{0,2},{2,0},{4,6},{6,4},{8,10},{10,8},{12,14},{14,12},{16,18},{18,... | collective-permute-start | bytes 589832 | tf_op jit(solution)/shard_map/ppermute | solution.py:82
  326.0 5.0 %collective-permute-start.37 = (f32[4608]{0:T(1024)}, f32[4608]{0:T(1024)}, u32[]{:S(2)}, u32[]{:S(2)}) collective-permute-start(f32[4608]{0:T(1024)} %add.628), channel_id=1, source_target_pairs={{0,4},{2,6},{4,0},{6,2},{8,12},{10,14},{12,8},{14,10},{16,20},{18,... | collective-permute-start | bytes 55304 | tf_op jit(solution)/shard_map/ppermute | solution.py:55
  332.4 6.4 %collective-permute-start.38 = (f32[4608]{0:T(1024)}, f32[4608]{0:T(1024)}, u32[]{:S(2)}, u32[]{:S(2)}) collective-permute-start(f32[4608]{0:T(1024)} %add.629), channel_id=1, source_target_pairs={{0,8},{2,10},{4,12},{6,14},{8,0},{10,2},{12,4},{14,6},{16,24},{18,... | collective-permute-start | bytes 55304 | tf_op jit(solution)/shard_map/ppermute | solution.py:55
  338.7 60.0 %collective-permute-start.20 = (f32[2,2,2,48,384]{4,3,1,0,2:T(8,128)S(1)}, f32[2,2,2,48,384]{4,3,1,0,2:T(8,128)S(1)}, u32[]{:S(2)}, u32[]{:S(2)}) collective-permute-start(f32[2,2,2,48,384]{4,3,1,0,2:T(8,128)S(1)} %bitcast.407), channel_id=1, source_target_pairs={{0,8},{2,10},{4,12},{6,14},{8,0},{10,2},{12,4},{14,6},{16,24},{18,... | collective-permute-start | bytes 1769480 | tf_op jit(solution)/shard_map/ppermute | solution.py:82
  339.6 6.9 %collective-permute-start.39 = (f32[4608]{0:T(1024)S(1)}, f32[4608]{0:T(1024)S(1)}, u32[]{:S(2)}, u32[]{:S(2)}) collective-permute-start(f32[4608]{0:T(1024)S(1)} %add.630), channel_id=1, source_target_pairs={{0,16},{2,18},{4,20},{6,22},{8,24},{10,26},{12,28},{14,30},{16,0},... | collective-permute-start | bytes 55304 | tf_op jit(solution)/shard_map/ppermute | solution.py:55
  346.4 54.3 %collective-permute-start.16 = (f32[2,2,2,48,384]{4,3,1,0,2:T(8,128)S(1)}, f32[2,2,2,48,384]{4,3,1,0,2:T(8,128)S(1)}, u32[]{:S(2)}, u32[]{:S(2)}) collective-permute-start(f32[2,2,2,48,384]{4,3,1,0,2:T(8,128)S(1)} %bitcast.408), channel_id=1, source_target_pairs={{0,4},{2,6},{4,0},{6,2},{8,12},{10,14},{12,8},{14,10},{16,20},{18,... | collective-permute-start | bytes 1769480 | tf_op jit(solution)/shard_map/ppermute | solution.py:82
  349.2 51.9 %collective-permute-start.12 = (f32[2,2,2,48,384]{4,3,1,0,2:T(8,128)S(1)}, f32[2,2,2,48,384]{4,3,1,0,2:T(8,128)S(1)}, u32[]{:S(2)}, u32[]{:S(2)}) collective-permute-start(f32[2,2,2,48,384]{4,3,1,0,2:T(8,128)S(1)} %bitcast.406), channel_id=1, source_target_pairs={{0,2},{2,0},{4,6},{6,4},{8,10},{10,8},{12,14},{14,12},{16,18},{18,... | collective-permute-start | bytes 1769480 | tf_op jit(solution)/shard_map/ppermute | solution.py:82
  351.6 71.7 %collective-permute-start.7 = (f32[1024,768]{1,0:T(8,128)S(1)}, f32[1024,768]{1,0:T(8,128)S(1)}, u32[]{:S(2)}, u32[]{:S(2)}) collective-permute-start(f32[1024,768]{1,0:T(8,128)S(1)} %copy-done.25), channel_id=1, source_target_pairs={{0,1},{1,0},{2,3},{3,2},{4,5},{5,4},{6,7},{7,6},{8,9},{9,8},{10,11... | collective-permute-start | bytes 9437192 | tf_op jit(solution)/shard_map/ppermute | solution.py:39
  352.7 8.7 %collective-permute-start.33 = (f32[2,2,48,128]{3,2,1,0:T(8,128)S(1)}, f32[2,2,48,128]{3,2,1,0:T(8,128)S(1)}, u32[]{:S(2)}, u32[]{:S(2)}) collective-permute-start(f32[2,2,48,128]{3,2,1,0:T(8,128)S(1)} %dynamic-slice_bitcast_fusion.24), channel_id=1, source_target_pairs={{0,2},{2,0},{4,6},{6,4},{8,10},{10,8},{12,14},{14,12},{16,18},{18,... | collective-permute-start | bytes 294920 | tf_op jit(solution)/shard_map/ppermute | solution.py:82
  361.5 4.8 %collective-permute-start.29 = (f32[2,2,48,128]{3,2,1,0:T(8,128)S(1)}, f32[2,2,48,128]{3,2,1,0:T(8,128)S(1)}, u32[]{:S(2)}, u32[]{:S(2)}) collective-permute-start(f32[2,2,48,128]{3,2,1,0:T(8,128)S(1)} %dynamic-slice_bitcast_fusion.25), channel_id=1, source_target_pairs={{0,2},{2,0},{4,6},{6,4},{8,10},{10,8},{12,14},{14,12},{16,18},{18,... | collective-permute-start | bytes 294920 | tf_op jit(solution)/shard_map/ppermute | solution.py:82
  366.3 4.6 %collective-permute-start.25 = (f32[2,2,48,128]{3,2,1,0:T(8,128)S(1)}, f32[2,2,48,128]{3,2,1,0:T(8,128)S(1)}, u32[]{:S(2)}, u32[]{:S(2)}) collective-permute-start(f32[2,2,48,128]{3,2,1,0:T(8,128)S(1)} %dynamic-slice_bitcast_fusion.26), channel_id=1, source_target_pairs={{0,4},{2,6},{4,0},{6,2},{8,12},{10,14},{12,8},{14,10},{16,20},{18,... | collective-permute-start | bytes 294920 | tf_op jit(solution)/shard_map/ppermute | solution.py:82
  370.9 4.1 collective-permute-start.34
  375.0 4.8 %collective-permute-start.30 = (f32[2,48,128]{2,1,0:T(8,128)S(1)}, f32[2,48,128]{2,1,0:T(8,128)S(1)}, u32[]{:S(2)}, u32[]{:S(2)}) collective-permute-start(f32[2,48,128]{2,1,0:T(8,128)S(1)} %dynamic-slice_bitcast_fusion.31), channel_id=1, source_target_pairs={{0,8},{2,10},{4,12},{6,14},{8,0},{10,2},{12,4},{14,6},{16,24},{18,... | collective-permute-start | bytes 147464 | tf_op jit(solution)/shard_map/ppermute | solution.py:82
  379.8 4.1 collective-permute-start.26
  383.9 4.7 %collective-permute-start.35 = (f32[48,128]{1,0:T(8,128)S(1)}, f32[48,128]{1,0:T(8,128)S(1)}, u32[]{:S(2)}, u32[]{:S(2)}) collective-permute-start(f32[48,128]{1,0:T(8,128)S(1)} %dynamic-slice_bitcast_fusion.33), channel_id=1, source_target_pairs={{0,16},{2,18},{4,20},{6,22},{8,24},{10,26},{12,28},{14,30},{16,0},... | collective-permute-start | bytes 73736 | tf_op jit(solution)/shard_map/ppermute | solution.py:82
  388.6 4.7 %collective-permute-start.31 = (f32[48,128]{1,0:T(8,128)S(1)}, f32[48,128]{1,0:T(8,128)S(1)}, u32[]{:S(2)}, u32[]{:S(2)}) collective-permute-start(f32[48,128]{1,0:T(8,128)S(1)} %dynamic-slice_bitcast_fusion.34), channel_id=1, source_target_pairs={{0,16},{2,18},{4,20},{6,22},{8,24},{10,26},{12,28},{14,30},{16,0},... | collective-permute-start | bytes 73736 | tf_op jit(solution)/shard_map/ppermute | solution.py:82
  393.4 4.7 %collective-permute-start.27 = (f32[48,128]{1,0:T(8,128)S(1)}, f32[48,128]{1,0:T(8,128)S(1)}, u32[]{:S(2)}, u32[]{:S(2)}) collective-permute-start(f32[48,128]{1,0:T(8,128)S(1)} %dynamic-slice_bitcast_fusion.35), channel_id=1, source_target_pairs={{0,16},{2,18},{4,20},{6,22},{8,24},{10,26},{12,28},{14,30},{16,0},... | collective-permute-start | bytes 73736 | tf_op jit(solution)/shard_map/ppermute | solution.py:82
  398.8 6.8 %collective-permute-start.21 = (f32[2,2,48,384]{3,2,1,0:T(8,128)S(1)}, f32[2,2,48,384]{3,2,1,0:T(8,128)S(1)}, u32[]{:S(2)}, u32[]{:S(2)}) collective-permute-start(f32[2,2,48,384]{3,2,1,0:T(8,128)S(1)} %dynamic-slice_bitcast_fusion.6), channel_id=1, source_target_pairs={{0,2},{2,0},{4,6},{6,4},{8,10},{10,8},{12,14},{14,12},{16,18},{18,... | collective-permute-start | bytes 884744 | tf_op jit(solution)/shard_map/ppermute | solution.py:82
  400.8 8.0 %collective-permute-start.17 = (f32[2,2,48,384]{3,2,1,0:T(8,128)S(1)}, f32[2,2,48,384]{3,2,1,0:T(8,128)S(1)}, u32[]{:S(2)}, u32[]{:S(2)}) collective-permute-start(f32[2,2,48,384]{3,2,1,0:T(8,128)S(1)} %dynamic-slice_bitcast_fusion.7), channel_id=1, source_target_pairs={{0,2},{2,0},{4,6},{6,4},{8,10},{10,8},{12,14},{14,12},{16,18},{18,... | collective-permute-start | bytes 884744 | tf_op jit(solution)/shard_map/ppermute | solution.py:82
  401.2 9.6 %collective-permute-start.13 = (f32[2,2,48,384]{3,2,1,0:T(8,128)S(1)}, f32[2,2,48,384]{3,2,1,0:T(8,128)S(1)}, u32[]{:S(2)}, u32[]{:S(2)}) collective-permute-start(f32[2,2,48,384]{3,2,1,0:T(8,128)S(1)} %dynamic-slice_bitcast_fusion.8), channel_id=1, source_target_pairs={{0,4},{2,6},{4,0},{6,2},{8,12},{10,14},{12,8},{14,10},{16,20},{18,... | collective-permute-start | bytes 884744 | tf_op jit(solution)/shard_map/ppermute | solution.py:82
  405.7 5.4 %collective-permute-start.22 = (f32[2,48,384]{2,1,0:T(8,128)S(1)}, f32[2,48,384]{2,1,0:T(8,128)S(1)}, u32[]{:S(2)}, u32[]{:S(2)}) collective-permute-start(f32[2,48,384]{2,1,0:T(8,128)S(1)} %dynamic-slice_bitcast_fusion.15), channel_id=1, source_target_pairs={{0,4},{2,6},{4,0},{6,2},{8,12},{10,14},{12,8},{14,10},{16,20},{18,... | collective-permute-start | bytes 442376 | tf_op jit(solution)/shard_map/ppermute | solution.py:82
  408.9 5.3 %collective-permute-start.18 = (f32[2,48,384]{2,1,0:T(8,128)S(1)}, f32[2,48,384]{2,1,0:T(8,128)S(1)}, u32[]{:S(2)}, u32[]{:S(2)}) collective-permute-start(f32[2,48,384]{2,1,0:T(8,128)S(1)} %dynamic-slice_bitcast_fusion.16), channel_id=1, source_target_pairs={{0,8},{2,10},{4,12},{6,14},{8,0},{10,2},{12,4},{14,6},{16,24},{18,... | collective-permute-start | bytes 442376 | tf_op jit(solution)/shard_map/ppermute | solution.py:82
  410.8 6.3 %collective-permute-start.14 = (f32[2,48,384]{2,1,0:T(8,128)S(1)}, f32[2,48,384]{2,1,0:T(8,128)S(1)}, u32[]{:S(2)}, u32[]{:S(2)}) collective-permute-start(f32[2,48,384]{2,1,0:T(8,128)S(1)} %dynamic-slice_bitcast_fusion.17), channel_id=1, source_target_pairs={{0,8},{2,10},{4,12},{6,14},{8,0},{10,2},{12,4},{14,6},{16,24},{18,... | collective-permute-start | bytes 442376 | tf_op jit(solution)/shard_map/ppermute | solution.py:82
  411.1 7.6 %collective-permute-start.23 = (f32[48,384]{1,0:T(8,128)S(1)}, f32[48,384]{1,0:T(8,128)S(1)}, u32[]{:S(2)}, u32[]{:S(2)}) collective-permute-start(f32[48,384]{1,0:T(8,128)S(1)} %dynamic-slice_bitcast_fusion.27), channel_id=1, source_target_pairs={{0,16},{2,18},{4,20},{6,22},{8,24},{10,26},{12,28},{14,30},{16,0},... | collective-permute-start | bytes 221192 | tf_op jit(solution)/shard_map/ppermute | solution.py:82
  414.2 5.4 %collective-permute-start.19 = (f32[48,384]{1,0:T(8,128)S(1)}, f32[48,384]{1,0:T(8,128)S(1)}, u32[]{:S(2)}, u32[]{:S(2)}) collective-permute-start(f32[48,384]{1,0:T(8,128)S(1)} %dynamic-slice_bitcast_fusion.28), channel_id=1, source_target_pairs={{0,16},{2,18},{4,20},{6,22},{8,24},{10,26},{12,28},{14,30},{16,0},... | collective-permute-start | bytes 221192 | tf_op jit(solution)/shard_map/ppermute | solution.py:82
  417.1 6.2 %collective-permute-start.15 = (f32[48,384]{1,0:T(8,128)S(1)}, f32[48,384]{1,0:T(8,128)S(1)}, u32[]{:S(2)}, u32[]{:S(2)}) collective-permute-start(f32[48,384]{1,0:T(8,128)S(1)} %dynamic-slice_bitcast_fusion.29), channel_id=1, source_target_pairs={{0,16},{2,18},{4,20},{6,22},{8,24},{10,26},{12,28},{14,30},{16,0},... | collective-permute-start | bytes 221192 | tf_op jit(solution)/shard_map/ppermute | solution.py:82
  425.6 3.8 collective-permute-start.8
  429.4 3.7 collective-permute-start.9
  433.1 3.7 collective-permute-start.10
  436.8 4.6 %collective-permute-start.11 = (f32[2304]{0:T(1024)S(1)}, f32[2304]{0:T(1024)S(1)}, u32[]{:S(2)}, u32[]{:S(2)}) collective-permute-start(f32[2304]{0:T(1024)S(1)} %add.588), channel_id=1, source_target_pairs={{0,16},{2,18},{4,20},{6,22},{8,24},{10,26},{12,28},{14,30},{16,0},... | collective-permute-start | bytes 27656 | tf_op jit(solution)/shard_map/ppermute | solution.py:55
  (71 other events, 772.5 us)

commit v2 on v0

v2 whole, which is shorter than its diff:
```python
import functools
import math

import jax
import jax.numpy as jnp
from jax import lax
from jax.experimental import pallas as pl
from jax.experimental.pallas import tpu as pltpu
from jax.sharding import PartitionSpec as P

HD = 64
NSTEPS = 2000
NB = 4
BLOCK = 256
PAIR = 2 * HD
VMEM_BYTES = 56 * 2**20

epsilon = 1e-05
F32 = jnp.float32
BF16 = jnp.bfloat16
NT = (((1,), (1,)), ((), ()))


def dot(left, right):
    return jnp.dot(left, right, preferred_element_type=F32)


def dot_nt(left, right):
    return lax.dot_general(left, right, NT, preferred_element_type=F32)


def row_mean(value):
    return jnp.mean(value, axis=-1, keepdims=True)


def column_sum(value):
    return jnp.sum(value, axis=0, keepdims=True)


def normed_of(source):
    centred = source - row_mean(source)
    inv_std = lax.rsqrt(row_mean(centred * centred) + epsilon)
    return centred * inv_std, inv_std


def accumulate(ref, value, first):
    @pl.when(first)
    def _():
        ref[...] = value

    @pl.when(jnp.logical_not(first))
    def _():
        ref[...] += value


def project_kernel(x_ref, time_ref, gain_ref, bias_ref, w_ref, qvb_ref, q_ref, k_ref, v_ref, at_ref):
    residual = x_ref[...].astype(F32) + time_ref[...]
    normed, _ = normed_of(residual)
    attn_in = (normed * gain_ref[...] + bias_ref[...]).astype(BF16)
    at_ref[...] = attn_in.T
    q_ref[...] = (dot(attn_in, w_ref[0]) + qvb_ref[0:1]).astype(BF16)
    k_ref[...] = dot(attn_in, w_ref[1]).astype(BF16)
    v_ref[...] = (dot(attn_in, w_ref[2]) + qvb_ref[1:2]).astype(BF16)


def head_mask(shape, head):
    lane = lax.broadcasted_iota(jnp.int32, shape, 1)
    return (lane >= HD) if head else (lane < HD)


def keep_head(value, head):
    return jnp.where(head_mask(value.shape, head), value, jnp.zeros_like(value))


EXP_SCALE = math.log2(math.e) / math.sqrt(HD)


def attend_kernel(q_ref, k_ref, v_ref, ow_ref, *refs):
    part_ref, mixed_ref, lse_ref, vt_ref = refs[-4:]

    @pl.when(pl.program_id(0) == 0)
    def _():
        vt_ref[...] = v_ref[...].T

    rows, width = q_ref.shape
    pieces = []
    stats = []
    for pair in range(width // PAIR):
        at = slice(pair * PAIR, (pair + 1) * PAIR)
        keys = k_ref[:, at]
        queries = q_ref[:, at]
        for head in range(2):
            scores = dot_nt(keys, keep_head(queries, head))
            top = jnp.max(scores, axis=0, keepdims=True)
            expo = jnp.exp2((scores - top) * EXP_SCALE)
            total = column_sum(expo)
            start = pair * PAIR + head * HD
            mixed = dot(vt_ref[start : start + HD, :], expo.astype(BF16))
            pieces.append(mixed * (1.0 / total))
            stats.append(top * EXP_SCALE + jnp.log2(total))
    while len(stats) < lse_ref.shape[0]:
        stats.append(jnp.zeros_like(stats[0]))
    lse_ref[...] = jnp.concatenate(stats, axis=0)
    mixed_heads = jnp.concatenate(pieces, axis=0).T.astype(BF16)
    mixed_ref[...] = mixed_heads
    part_ref[...] = dot(mixed_heads, ow_ref[...])


def normal_parts(v):
    size = jnp.abs(v)
    t = 1.0 / (1.0 + 0.2316419 * size)
    poly = t * (
        0.319381530
        + t * (-0.356563782 + t * (1.781477937 + t * (-1.821255978 + t * 1.330274429)))
    )
    density = jnp.exp2(v * v * (-0.5 * math.log2(math.e))) * (1.0 / math.sqrt(2.0 * math.pi))
    tail = poly * density
    return jnp.where(v < 0.0, tail, 1.0 - tail), density


def feed_kernel(
    x_ref, time_ref, own_ref, got_ref, ob_ref, gain_ref, bias_ref, uw_ref, ub_ref, dw_ref, *refs
):
    part_ref, mid_ref, ft_ref, act_ref, slope_ref = refs[-5:]
    mid = x_ref[...].astype(F32) + time_ref[...] + (own_ref[...] + got_ref[...]) + ob_ref[...]
    mid_ref[...] = mid
    normed, _ = normed_of(mid)
    ffn_in = (normed * gain_ref[...] + bias_ref[...]).astype(BF16)
    ft_ref[...] = ffn_in.T
    preact = dot(ffn_in, uw_ref[...]) + ub_ref[...]
    phi, density = normal_parts(preact)
    activated = (preact * phi).astype(BF16)
    act_ref[...] = activated
    slope_ref[...] = phi + preact * density
    part_ref[...] = dot(activated, dw_ref[...])


def loss_kernel(mid_ref, own_ref, got_ref, db_ref, goal_ref, weight_ref, *refs):
    sum_ref, out_ref, og_ref, low_ref, lt_ref = refs[-5:]
    final = mid_ref[...] + (own_ref[...] + got_ref[...]) + db_ref[...]
    out_ref[...] = final.astype(BF16)
    out_grad = (final - goal_ref[...].astype(F32)) * weight_ref[0, 0]
    og_ref[...] = out_grad
    low = out_grad.astype(BF16)
    low_ref[...] = low
    lt_ref[...] = low.T
    accumulate(sum_ref, column_sum(out_grad), pl.program_id(0) == 0)


def back_feed_kernel(low_ref, slope_ref, uw_ref, dw_ref, pre_ref, part_ref, sum_ref):
    pre_grad = slope_ref[...] * dot_nt(low_ref[...], dw_ref[...])
    accumulate(sum_ref, column_sum(pre_grad), pl.program_id(0) == 0)
    low = pre_grad.astype(BF16)
    pre_ref[...] = low
    part_ref[...] = dot_nt(low, uw_ref[...])


def back_mid_kernel(
    mid_ref, own_ref, got_ref, og_ref, gain_ref, ow_ref,
    mg_ref, mt_ref, mixed_ref, gain_sum_ref, bias_sum_ref, out_sum_ref,
):
    first = pl.program_id(0) == 0
    normed, inv_std = normed_of(mid_ref[...])
    upstream = own_ref[...] + got_ref[...]
    scaled = upstream * gain_ref[...]
    inner = scaled - row_mean(scaled) - normed * row_mean(scaled * normed)
    mid_grad = og_ref[...] + inv_std * inner
    mg_ref[...] = mid_grad
    low = mid_grad.astype(BF16)
    mt_ref[...] = low.T
    mixed_ref[...] = dot_nt(low, ow_ref[...]).astype(BF16)
    accumulate(gain_sum_ref, column_sum(upstream * normed), first)
    accumulate(bias_sum_ref, column_sum(upstream), first)
    accumulate(out_sum_ref, column_sum(mid_grad), first)


def back_attend_kernel(
    pair, q_ref, k_ref, v_ref, do_ref, o_ref, lse_ref,
    dq_ref, dk_ref, dv_ref, dq_sum_ref, dv_sum_ref, kt_ref, dk_acc, dv_acc,
):
    step = pl.program_id(0)
    scale = 1.0 / math.sqrt(HD)

    @pl.when(step == 0)
    def _():
        kt_ref[...] = k_ref[...].T
        dk_acc[...] = jnp.zeros_like(dk_acc)
        dv_acc[...] = jnp.zeros_like(dv_acc)

    keys, values, queries, upstream = k_ref[...], v_ref[...], q_ref[...], do_ref[...]
    both = (upstream.astype(F32) * o_ref[...].astype(F32)).T
    pieces = []
    for head in range(2):
        own_queries = keep_head(queries, head)
        own_upstream = keep_head(upstream, head)
        row_dot = column_sum(both[head * HD : (head + 1) * HD])
        log_total = lse_ref[2 * pair + head : 2 * pair + head + 1, :]
        scores = dot_nt(keys, own_queries)
        probs = jnp.exp2(scores * EXP_SCALE - log_total)
        prob_grad = dot_nt(values, own_upstream)
        score_grad = (probs * (prob_grad - row_dot)).astype(BF16)
        dv_acc[...] += dot(probs.astype(BF16), own_upstream)
        dk_acc[...] += dot(score_grad, own_queries)
        pieces.append(dot(kt_ref[head * HD : (head + 1) * HD, :], score_grad))
    query_grad = jnp.concatenate(pieces, axis=0).T * scale
    dq_ref[...] = query_grad.astype(BF16)
    accumulate(dq_sum_ref, column_sum(query_grad), step == 0)

    @pl.when(step == pl.num_programs(0) - 1)
    def _():
        dk_ref[...] = (dk_acc[...] * scale).astype(BF16)
        dv = dv_acc[...]
        dv_ref[...] = dv.astype(BF16)
        dv_sum_ref[...] = column_sum(dv)


def back_project_kernel(*refs):
    w_ref, part_ref = refs[-2:]
    pairs = (len(refs) - 2) // 3
    total = None
    for kind in range(3):
        grad = jnp.concatenate([refs[3 * pair + kind][...] for pair in range(pairs)], axis=1)
        term = dot_nt(grad, w_ref[kind])
        total = term if total is None else total + term
    part_ref[...] = total


def back_input_kernel(
    x_ref, time_ref, own_ref, got_ref, mg_ref, gain_ref,
    out_ref, time_sum_ref, gain_sum_ref, bias_sum_ref,
):
    first = pl.program_id(0) == 0
    normed, inv_std = normed_of(x_ref[...].astype(F32) + time_ref[...])
    upstream = own_ref[...] + got_ref[...]
    scaled = upstream * gain_ref[...]
    inner = scaled - row_mean(scaled) - normed * row_mean(scaled * normed)
    grad = mg_ref[...] + inv_std * inner
    out_ref[...] = grad
    accumulate(time_sum_ref, column_sum(grad), first)
    accumulate(gain_sum_ref, column_sum(upstream * normed), first)
    accumulate(bias_sum_ref, column_sum(upstream), first)


def weight_kernel(chunk, count, from_ref, *refs):
    keep_ref, send_ref, whole_ref = refs[-3:]
    xt_ref = refs[0]
    total = None
    parts = [ref[...] for ref in refs[1:-3]]
    right = parts[0] if len(parts) == 1 else jnp.concatenate(parts, axis=1)
    whole_ref[...] = dot(xt_ref[...], right)
    for place in range(count):
        start = pl.multiple_of(from_ref[place] * chunk, 8)
        rows = whole_ref[pl.ds(start, chunk), :]
        half = count // 2
        target = keep_ref if place < half else send_ref
        at = (place % half) * chunk
        target[at : at + chunk, :] = rows


def whole_weight_kernel(xt_ref, *refs):
    parts = [ref[...] for ref in refs[:-1]]
    right = parts[0] if len(parts) == 1 else jnp.concatenate(parts, axis=1)
    refs[-1][...] = dot(xt_ref[...], right)


def fixed(shape):
    return pl.BlockSpec(shape, lambda *_: (0,) * len(shape))


def by_rows(width, offset=0, rows=BLOCK):
    return pl.BlockSpec((rows, width), lambda step: (step + offset, 0))


def by_columns(height, offset=0, columns=BLOCK):
    return pl.BlockSpec((height, columns), lambda step: (0, step + offset))


def shaped(shape, dtype):
    return jax.ShapeDtypeStruct(shape, dtype)


def call(name, kernel, grid, args, specs, outs, out_specs, scratch=(), flops=0, prior=None):
    prior = list(prior or [])
    aliases = {}
    for place in range(len(prior)):
        aliases[len(args) + place] = len(outs) - len(prior) + place
    moved = sum(math.prod(a.shape) * a.dtype.itemsize for a in [*args, *outs])
    return pl.pallas_call(
        kernel,
        name=name,
        grid=grid,
        in_specs=[*specs, *[pl.BlockSpec(memory_space=pl.ANY) for _ in prior]],
        out_specs=out_specs,
        out_shape=outs,
        scratch_shapes=list(scratch),
        input_output_aliases=aliases,
        compiler_params=pltpu.CompilerParams(vmem_limit_bytes=VMEM_BYTES),
        cost_estimate=pl.CostEstimate(flops=int(flops), bytes_accessed=int(moved), transcendentals=0),
    )(*args, *prior)


def swap(value):
    return lax.ppermute(value, "mp", [(0, 1), (1, 0)])


def xor_pairs(size, bit):
    return [(index, index ^ bit) for index in range(size)]


def axis_bits(size):
    return [1 << place for place in range(size.bit_length() - 1)]


def hop(value, bit):
    return lax.ppermute(value, "dp", xor_pairs(lax.axis_size("dp"), bit))


def double_sum(value):
    for bit in axis_bits(lax.axis_size("dp")):
        value = value + hop(value, bit)
    return value


def halve(section, order):
    size = lax.axis_size("dp")
    me = lax.axis_index("dp")
    left = sorted(order, reverse=True)
    rows, columns = section.shape
    section = section.reshape((2,) * len(left) + (rows // size, columns))
    for bit in order:
        at = left.index(bit)
        mine = (me // bit) % 2
        send = lax.dynamic_index_in_dim(section, 1 - mine, at, keepdims=False)
        keep = lax.dynamic_index_in_dim(section, mine, at, keepdims=False)
        section = keep + hop(send, bit)
        left.remove(bit)
    return section


def chunk_sources(order):
    me = lax.axis_index("dp")
    places = []
    for place in range(1 << len(order)):
        relative = 0
        for step, bit in enumerate(order):
            if (place >> (len(order) - 1 - step)) & 1:
                relative |= bit
        places.append(relative)
    return jnp.array(places, jnp.int32) ^ me


class Section:
    def __init__(self, order, keep, send):
        self.order = list(order)
        self.keep = keep
        self.send = send

    def step(self, got=None):
        got = hop(self.send, self.order[0]) if got is None else got
        self.order = self.order[1:]
        if not self.order:
            self.keep = self.keep + got
            self.send = None
            return
        half = self.keep.shape[0] // 2
        self.send = self.keep[half:] + got[half:]
        self.keep = self.keep[:half] + got[:half]


def joint_step(sections):
    widths = [section.send.shape[1] for section in sections]
    got = hop(jnp.concatenate([section.send for section in sections], axis=1), sections[0].order[0])
    start = 0
    for section, width in zip(sections, widths):
        section.step(got[:, start : start + width])
        start += width


def weight_section(name, xt, parts, starts, width, order, block):
    size = lax.axis_size("dp")
    model, tokens = xt.shape
    chunk = model // size
    steps = width // block
    each = block // len(parts)
    flops = 2 * model * tokens * width
    y_specs = [by_columns(tokens, start // each, each) for start in starts]
    x_spec = fixed(xt.shape)
    if chunk % 8:
        whole = call(
            name, whole_weight_kernel, (steps,), [xt, *parts], [x_spec, *y_specs],
            [shaped((model, width), F32)], [by_columns(model, 0, block)], flops=flops,
        )[0]
        section = Section([], halve(whole, order), None)
        return section
    half = shaped((model // 2, width), F32)
    keep, send = pl.pallas_call(
        functools.partial(weight_kernel, chunk, size),
        name=name,
        grid_spec=pltpu.PrefetchScalarGridSpec(
            num_scalar_prefetch=1,
            grid=(steps,),
            in_specs=[
                pl.BlockSpec(xt.shape, lambda step, _: (0, 0)),
                *[
                    pl.BlockSpec((tokens, each), lambda step, _, at=start // each: (0, step + at))
                    for start in starts
                ],
            ],
            out_specs=[pl.BlockSpec((model // 2, block), lambda step, _: (0, step))] * 2,
            scratch_shapes=[pltpu.VMEM((model, block), F32)],
        ),
        out_shape=[half, half],
        compiler_params=pltpu.CompilerParams(vmem_limit_bytes=VMEM_BYTES),
        cost_estimate=pl.CostEstimate(
            flops=flops, bytes_accessed=2 * model * tokens + 2 * tokens * width + 4 * model * width,
            transcendentals=0,
        ),
    )(chunk_sources(order), xt, *parts)
    return Section(order, keep, send)


def section_orders(size):
    bits = axis_bits(size)
    if len(bits) == 4:
        x_bit, y_bit, z_low, z_high = bits
        return {
            "xy": [x_bit, y_bit, z_low, z_high],
            "yx": [y_bit, x_bit, z_low, z_high],
            "zxy": [z_low, x_bit, y_bit, z_high],
            "zyx": [z_low, y_bit, x_bit, z_high],
        }
    count = len(bits)
    turn = lambda start: bits[start % count :] + bits[: start % count]
    return {"xy": turn(0), "yx": turn(1), "zxy": turn(2), "zyx": turn(3)}


def local(
    inputs,
    time_embed,
    targets,
    timesteps,
    ln1_gain,
    ln1_bias,
    qkv_weight,
    qv_bias,
    out_weight,
    out_bias,
    ln2_gain,
    ln2_bias,
    up_weight,
    up_bias,
    down_weight,
    down_bias,
):
    seq_count, length, model = inputs.shape
    width = qkv_weight.shape[2]
    hidden = up_weight.shape[1]
    blocks = length // BLOCK
    halves = 2
    per_half = blocks // halves
    pairs = width // PAIR
    x = inputs.reshape(length, model)
    goal = targets.reshape(length, model)
    w_qkv = jnp.transpose(qkv_weight, (1, 0, 2))
    row = lambda vector: vector.reshape(1, -1)
    g1, b1, g2, b2 = row(ln1_gain), row(ln1_bias), row(ln2_gain), row(ln2_bias)
    ob, ub, db = row(out_bias), row(up_bias), row(down_bias)

    buckets = (
        (timesteps >= NSTEPS // 64).astype(jnp.int32)
        + (timesteps >= NSTEPS // 16).astype(jnp.int32)
        + (timesteps >= NSTEPS // 4).astype(jnp.int32)
    )
    one_hot = buckets[:, None] == jnp.arange(NB, dtype=jnp.int32)[None, :]
    bucket_counts = double_sum(jnp.sum(one_hot.astype(jnp.int32), axis=0))
    floors = jnp.maximum(bucket_counts, 1).astype(F32)
    total_seqs = seq_count * lax.axis_size("dp")
    seq_weight = total_seqs / (NB * jnp.sum(jnp.where(one_hot, floors[None, :], 0.0), axis=1))
    weight = seq_weight.reshape(1, 1)

    vec = fixed((1, model))
    mat = shaped((length, model), F32)
    low_mat = shaped((length, model), BF16)
    low_t = shaped((model, length), BF16)

    q, k, v, attn_t = call(
        "project", project_kernel, (blocks,),
        [x, time_embed, g1, b1, w_qkv, qv_bias],
        [by_rows(model), vec, vec, vec, fixed(w_qkv.shape), fixed(qv_bias.shape)],
        [shaped((length, width), BF16)] * 3 + [low_t],
        [by_rows(width)] * 3 + [by_columns(model)],
        flops=6 * length * model * width,
    )

    half_mat = shaped((length // halves, model), F32)
    prior = None
    own_attn, got_attn = [], []
    for half in range(halves):
        at = half * per_half
        part, *prior = call(
            "attend", attend_kernel, (per_half,),
            [q, k, v, out_weight],
            [by_rows(width, at), fixed(k.shape), fixed(v.shape), fixed(out_weight.shape)],
            [half_mat, shaped((length, width), BF16), shaped((8, length), F32)],
            [by_rows(model), by_rows(width, at), by_columns(8, at)],
            scratch=[pltpu.VMEM((width, length), BF16)],
            flops=16 * length * length * width // halves, prior=prior,
        )
        own_attn.append(part)
        got_attn.append(swap(part))
    mixed, lse = prior

    prior = None
    own_feed, got_feed = [], []
    for half in range(halves):
        at = half * per_half
        part, *prior = call(
            "feed", feed_kernel, (per_half,),
            [x, time_embed, own_attn[half], got_attn[half], ob, g2, b2, up_weight, ub, down_weight],
            [by_rows(model, at), vec, by_rows(model), by_rows(model), vec, vec, vec,
             fixed(up_weight.shape), fixed(ub.shape), fixed(down_weight.shape)],
            [half_mat, mat, low_t, shaped((length, hidden), BF16), shaped((length, hidden), F32)],
            [by_rows(model), by_rows(model, at), by_columns(model, at), by_rows(hidden, at),
             by_rows(hidden, at)],
            flops=4 * length * model * hidden // halves, prior=prior,
        )
        own_feed.append(part)
        got_feed.append(swap(part))
    mid, feed_t, activated, slope = prior

    prior = None
    down_sums = []
    for half in range(halves):
        at = half * per_half
        total, *prior = call(
            "loss", loss_kernel, (per_half,),
            [mid, own_feed[half], got_feed[half], db, goal, weight],
            [by_rows(model, at), by_rows(model), by_rows(model), vec, by_rows(model, at),
             pl.BlockSpec(memory_space=pltpu.SMEM)],
            [shaped((1, model), F32), low_mat, mat, low_mat, low_t],
            [vec, by_rows(model, at), by_rows(model, at), by_rows(model, at), by_columns(model, at)],
            prior=prior,
        )
        down_sums.append(total)
    out_act, out_grad, out_low, out_t = prior

    orders = section_orders(lax.axis_size("dp"))
    third = hidden // 2
    down_a = weight_section("grad_down", out_t, [activated], [0], third, orders["xy"], 256)
    down_b = weight_section("grad_down", out_t, [activated], [third], third, orders["yx"], 256)

    pre_low, own_pre, up_sum = call(
        "back_feed", back_feed_kernel, (blocks,),
        [out_low, slope, up_weight, down_weight],
        [by_rows(model), by_rows(hidden), fixed(up_weight.shape), fixed(down_weight.shape)],
        [shaped((length, hidden), BF16), mat, shaped((1, hidden), F32)],
        [by_rows(hidden), by_rows(model), fixed((1, hidden))],
        flops=4 * length * model * hidden,
    )
    got_pre = swap(own_pre)
    up_a = weight_section("grad_up", feed_t, [pre_low], [0], third, orders["zxy"], 256)
    up_b = weight_section("grad_up", feed_t, [pre_low], [third], third, orders["zyx"], 256)

    mid_grad, mid_t, mixed_grad, gain2_sum, bias2_sum, out_sum = call(
        "back_mid", back_mid_kernel, (blocks,),
        [mid, own_pre, got_pre, out_grad, g2, out_weight],
        [by_rows(model)] * 4 + [vec, fixed(out_weight.shape)],
        [mat, low_t, shaped((length, width), BF16)] + [shaped((1, model), F32)] * 3,
        [by_rows(model), by_columns(model), by_rows(width)] + [vec] * 3,
        flops=2 * length * model * width,
    )
    out_s = weight_section("grad_out", mid_t, [mixed], [0], width, orders["xy"], 128)

    grads, sums, qkv_s = [], [], []
    for pair in range(pairs):
        at_rows = pl.BlockSpec((BLOCK, PAIR), lambda step, pair=pair: (step, pair))
        whole = pl.BlockSpec((length, PAIR), lambda step, pair=pair: (0, pair))
        one = shaped((length, PAIR), BF16)
        one_sum = shaped((1, PAIR), F32)
        dq, dk, dv, dq_sum, dv_sum = call(
            "back_attend", functools.partial(back_attend_kernel, pair), (blocks,),
            [q, k, v, mixed_grad, mixed, lse],
            [at_rows, whole, whole, at_rows, at_rows, by_columns(8)],
            [one, one, one, one_sum, one_sum],
            [by_rows(PAIR), fixed((length, PAIR)), fixed((length, PAIR)), fixed((1, PAIR)),
             fixed((1, PAIR))],
            scratch=[pltpu.VMEM((PAIR, length), BF16), pltpu.VMEM((length, PAIR), F32),
                     pltpu.VMEM((length, PAIR), F32)],
            flops=40 * length * length * PAIR,
        )
        grads += [dq, dk, dv]
        sums.append((dq_sum, dv_sum))
        order = orders["yx"] if pair % 2 == 0 else orders["xy"]
        qkv_s.append(
            weight_section("grad_qkv", attn_t, [dq, dk, dv], [0, 0, 0], 3 * PAIR, order, 3 * PAIR)
        )

    own_proj = call(
        "back_project", back_project_kernel, (blocks,),
        [*grads, w_qkv], [by_rows(PAIR)] * len(grads) + [fixed(w_qkv.shape)],
        [mat], [by_rows(model)], flops=6 * length * model * width,
    )[0]
    got_proj = swap(own_proj)
    input_grad, grad_time, gain1_sum, bias1_sum = call(
        "back_input", back_input_kernel, (blocks,),
        [x, time_embed, own_proj, got_proj, mid_grad, g1],
        [by_rows(model), vec, by_rows(model), by_rows(model), by_rows(model), vec],
        [mat] + [shaped((1, model), F32)] * 3,
        [by_rows(model)] + [vec] * 3,
    )

    early = jnp.concatenate(
        [out_sum, gain2_sum, bias2_sum, up_sum, down_sums[0] + down_sums[1]], axis=1
    )
    late = jnp.concatenate(
        [gain1_sum, bias1_sum, *[s[0] for s in sums], *[s[1] for s in sums]], axis=1
    )
    early = double_sum(early)[0]
    late = double_sum(late)[0]

    for section in (down_a, down_b, up_a, up_b, out_s, *qkv_s):
        while section.order:
            section.step()

    qkv_part = jnp.concatenate([s.keep.reshape(-1, 3, PAIR) for s in qkv_s], axis=2)
    return (
        out_act.reshape(inputs.shape),
        input_grad.reshape(inputs.shape),
        grad_time,
        late[:model],
        late[model : 2 * model],
        qkv_part,
        late[2 * model :].reshape(2, width),
        out_s.keep.T,
        early[:model],
        early[model : 2 * model],
        early[2 * model : 3 * model],
        jnp.concatenate([up_a.keep, up_b.keep], axis=1),
        early[3 * model : 3 * model + hidden],
        jnp.concatenate([down_a.keep, down_b.keep], axis=1).T,
        early[3 * model + hidden :],
        bucket_counts,
    )


def solution(mesh):
    in_specs = (
        P("dp", None, None),
        P("dp", None),
        P("dp", None, None),
        P("dp"),
        P(),
        P(),
        P(None, None, "mp"),
        P(None, "mp"),
        P("mp", None),
        P(),
        P(),
        P(),
        P(None, "mp"),
        P("mp"),
        P("mp", None),
        P(),
    )
    out_specs = (
        P("dp", None, None),
        P("dp", None, None),
        P("dp", None),
        P(),
        P(),
        P("dp", None, "mp"),
        P(None, "mp"),
        P("mp", "dp"),
        P(),
        P(),
        P(),
        P("dp", "mp"),
        P("mp"),
        P("mp", "dp"),
        P(),
        P(),
    )
    return jax.shard_map(local, mesh=mesh, in_specs=in_specs, out_specs=out_specs, check_vma=False)
```

time: 837 us -> 344 us (0.41)
  waiting for transfers between devices: 517 us -> 89.7 us
  Pallas kernels: 0 us -> 162 us
  matrix products: 123 us -> 0 us
  blocking collectives: 92.5 us -> 0 us
  starting transfers between devices: 0.54 us -> 60.1 us
  other arithmetic: 65.7 us -> 10.7 us
  between operations: 16.5 us -> 2.57 us
    reduce_scatter x4 -> x0, waiting for transfers between devices: 459 us -> none  [the longest x1 142 us: local(): lax.psum_scatter(grad_up, 'dp', scatter_dimension=0, tiled=True)]
    pallas_call x0 -> x22, Pallas kernels: none -> 162 us  [the longest x14 120 us: call(): pl.pallas_call(kernel, name=name, grid=grid, in_specs=[*specs, *[pl.Block...]
    dot_general x24 -> x0, matrix products: 123 us -> none  [the longest x1 17.6 us: local(): jnp.dot(ffn_in, up_weight, preferred_element_type=jnp.float32) + up_bias]
    psum x2 -> x0, blocking collectives: 92.5 us -> none  [the longest x1 77.8 us: local(): lax.psum((grad_ln1_gain, grad_ln1_bias, qv_bias_grad, jnp.sum(mid_grad, a...]
    ppermute x0 -> x50, waiting for transfers between devices: none -> 89.7 us  [the longest x44 89.7 us: hop(): return lax.ppermute(value, 'dp', xor_pairs(lax.axis_size('dp'), bit))]
    ppermute x0 -> x50, starting transfers between devices: none -> 60.1 us  [the longest x44 58.9 us: hop(): return lax.ppermute(value, 'dp', xor_pairs(lax.axis_size('dp'), bit))]
    psum x4 -> x0, waiting for transfers between devices: 58.3 us -> none  [the longest x1 26 us: local(): lax.psum(jnp.dot(mixed_heads, out_weight, preferred_element_type=jnp.floa...]
    reduce_sum x13 -> x0, other arithmetic: 43.5 us -> none  [the longest x2 10.3 us: local(): row_total = jnp.sum(expo_vals, axis=-1, keepdims=True)]
  transfers between devices with their start and end apart: 8 -> 50, of which waited for: 7 -> 25; matrix products, arithmetic and copies ran while one was open for 4% -> 5% of each run, Pallas kernels for 0% -> 27%
where the time goes in v2:
time: 344 us; the launch traced here: 343 us
  Pallas kernels  162 us (47%)
  waiting for transfers between devices  89.7 us (26%)
  starting transfers between devices  60.1 us (17%)
  local copies, waits for them, and re-layouts  18.3 us (5%)
  other arithmetic  10.7 us (3%)
    pallas_call x14, Pallas kernels, call(): pl.pallas_call(kernel, name=name, grid=grid, in_specs=[*specs, *[pl.Block...  120 us
    ppermute x44, waiting for transfers between devices, hop(): return lax.ppermute(value, 'dp', xor_pairs(lax.axis_size('dp'), bit))  89.7 us
    ppermute x44, starting transfers between devices, hop(): return lax.ppermute(value, 'dp', xor_pairs(lax.axis_size('dp'), bit))  58.9 us
    pallas_call x8, Pallas kernels, weight_section(): pl.pallas_call(functools.partial(weight_kernel, chunk, size), name=name,...  41.8 us
    unnamed x84, local copies, waits for them, and re-layouts  10.3 us
  transfers between devices with their start and end apart: 50, of which 25 were waited for; matrix products, arithmetic and copies ran while one was open for 5% of the time, Pallas kernels for 27%

profile of v2, /device:TPU:0, one launch (start us, length us, event | category | flops | bytes accessed | tf_op | source)
XLA Modules:
  0.0 343.2 jit_solution(11565340434381401069)
XLA Ops:
  3.2 6.6 %project.1 = (bf16[1024,384]{1,0:T(8,128)(2,1)}, bf16[1024,384]{1,0:T(8,128)(2,1)}, bf16[1024,384]{1,0:T(8,128)(2,1)}, bf16[768,1024]{1,0:T(8,128)(2,1)}) custom-call(bf16[1024,768]{1,0:T(8,128)(2,1)} %bitcast.11, f32[1,768]{1,0:T(1,128)} %time_ref.7, f32[1,768]{1,0:T(1,128)} %reshape.105.gain_ref, f32[1,768]{1,0:T(1,128)} %reshape.106.bias_ref, ...), custom_call_target="tpu_custom_call" | custom-call | flops 1811939328 | bytes 7286784 | tf_op jit(solution)/shard_map/project/pallas_call | solution.py:288
  9.8 12.0 %attend.2 = (f32[512,768]{1,0:T(8,128)}, bf16[1024,384]{1,0:T(8,128)(2,1)}, f32[8,1024]{1,0:T(8,128)}) custom-call(bf16[1024,384]{1,0:T(8,128)(2,1)} %get-tuple-element.90.q_ref, bf16[1024,384]{1,0:T(8,128)(2,1)} %get-tuple-element.91.k_ref, bf16[1024,384]{1,0:T(8,128)(2,1)} %get-tuple-element.92.v_ref, bf16[384,768]{1,0:T(8,128)(2,1)} %ow_ref.5), custom_call_target="tpu_custom_call" | custom-call | flops 3221225472 | bytes 5341184 | tf_op jit(solution)/shard_map/attend/pallas_call | solution.py:288
  22.3 12.1 %attend.3 = (f32[512,768]{1,0:T(8,128)}, bf16[1024,384]{1,0:T(8,128)(2,1)}, f32[8,1024]{1,0:T(8,128)}) custom-call(bf16[1024,384]{1,0:T(8,128)(2,1)} %get-tuple-element.90.q_ref, bf16[1024,384]{1,0:T(8,128)(2,1)} %get-tuple-element.91.k_ref, bf16[1024,384]{1,0:T(8,128)(2,1)} %get-tuple-element.92.v_ref, ...), custom_call_target="tpu_custom_call", output_to_operand_aliasing={{1}: (4, {}), {2}: (5, {})} | custom-call | flops 3221225472 | bytes 5341184 | tf_op jit(solution)/shard_map/attend/pallas_call | solution.py:288
  37.9 9.8 %feed.2 = (f32[512,768]{1,0:T(8,128)}, f32[1024,768]{1,0:T(8,128)}, bf16[768,1024]{1,0:T(8,128)(2,1)}, bf16[1024,1536]{1,0:T(8,128)(2,1)}, f32[1024,1536]{1,0:T(8,128)}) custom-call(bf16[1024,768]{1,0:T(8,128)(2,1)} %bitcast.12, f32[1,768]{1,0:T(1,128)} %time_ref.7, f32[512,768]{1,0:T(8,128)} %get-tuple-element.96.own_ref, f32[512,768]{1,0:T(8,128)} %copy-done.6, ...), custom_call_target="tpu_custom_call" | custom-call | flops 2415919104 | bytes 25184256 | tf_op jit(solution)/shard_map/feed/pallas_call | solution.py:288
  49.4 9.8 %feed.3 = (f32[512,768]{1,0:T(8,128)}, f32[1024,768]{1,0:T(8,128)}, bf16[768,1024]{1,0:T(8,128)(2,1)}, bf16[1024,1536]{1,0:T(8,128)(2,1)}, f32[1024,1536]{1,0:T(8,128)}) custom-call(bf16[1024,768]{1,0:T(8,128)(2,1)} %bitcast.13, f32[1,768]{1,0:T(1,128)} %time_ref.7, ...), custom_call_target="tpu_custom_call", output_to_operand_aliasing={{1}: (10, {}), {2}: (11, {}), {3}: (12, {}), {4}: (13, {})} | custom-call | flops 2415919104 | bytes 25184256 | tf_op jit(solution)/shard_map/feed/pallas_call | solution.py:288
  60.1 3.0 collective-permute-start.3
  65.2 1.6 collective-permute-start.4
  66.8 2.0 collective-permute-done.4
  68.8 1.6 collective-permute-start.5
  70.4 2.0 collective-permute-done.5
  72.4 2.6 collective-permute-start.6
  75.0 1.8 collective-permute-done.6
  79.8 4.2 %loss.2 = (f32[1,768]{1,0:T(1,128)}, bf16[1024,768]{1,0:T(8,128)(2,1)}, f32[1024,768]{1,0:T(8,128)}, bf16[1024,768]{1,0:T(8,128)(2,1)}, bf16[768,1024]{1,0:T(8,128)(2,1)}) custom-call(f32[1024,768]{1,0:T(8,128)} %get-tuple-element.101.mid_ref, f32[512,768]{1,0:T(8,128)} %get-tuple-element.103.own_ref, f32[512,768]{1,0:T(8,128)} %copy-done.5, ...), custom_call_target="tpu_custom_call" | custom-call | bytes 15734788 | tf_op jit(solution)/shard_map/loss/pallas_call | solution.py:288
  85.1 4.2 %loss.3 = (f32[1,768]{1,0:T(1,128)}, bf16[1024,768]{1,0:T(8,128)(2,1)}, f32[1024,768]{1,0:T(8,128)}, bf16[1024,768]{1,0:T(8,128)(2,1)}, bf16[768,1024]{1,0:T(8,128)(2,1)}) custom-call(f32[1024,768]{1,0:T(8,128)} %get-tuple-element.101.mid_ref, ...), custom_call_target="tpu_custom_call", output_to_operand_aliasing={{1}: (6, {}), {2}: (7, {}), {3}: (8, {}), {4}: (9, {})} | custom-call | bytes 15734788 | tf_op jit(solution)/shard_map/loss/pallas_call | solution.py:288
  89.4 5.7 %grad_down.2 = (f32[384,768]{1,0:T(8,128)}, f32[384,768]{1,0:T(8,128)}) custom-call(s32[16]{0:T(128)} %broadcast_xor_fusion.2.from_ref, bf16[768,1024]{1,0:T(8,128)(2,1)} %get-tuple-element.158.refs_0_, bf16[1024,1536]{1,0:T(8,128)(2,1)} %get-tuple-element.159.refs_1_), custom_call_target="tpu_custom_call" | custom-call | flops 1207959552 | bytes 5505024 | tf_op jit(solution)/shard_map/grad_down/pallas_call | solution.py:396
  96.4 5.8 %grad_down.3 = (f32[384,768]{1,0:T(8,128)}, f32[384,768]{1,0:T(8,128)}) custom-call(s32[16]{0:T(128)} %broadcast_xor_fusion.3.from_ref, bf16[768,1024]{1,0:T(8,128)(2,1)} %get-tuple-element.158.refs_0_, bf16[1024,1536]{1,0:T(8,128)(2,1)} %get-tuple-element.159.refs_1_), custom_call_target="tpu_custom_call" | custom-call | flops 1207959552 | bytes 5505024 | tf_op jit(solution)/shard_map/grad_down/pallas_call | solution.py:396
  102.2 1.5 collective-permute-start.46
  103.7 12.3 %back_feed.1 = (bf16[1024,1536]{1,0:T(8,128)(2,1)}, f32[1024,768]{1,0:T(8,128)}, f32[1,1536]{1,0:T(1,128)}) custom-call(bf16[1024,768]{1,0:T(8,128)(2,1)} %get-tuple-element.109.low_ref, f32[1024,1536]{1,0:T(8,128)} %get-tuple-element.110.slope_ref, bf16[768,1536]{1,0:T(8,128)(2,1)} %uw_ref.5, bf16[1536,768]{1,0:T(8,128)(2,1)} %dw_ref.5), custom_call_target="tpu_custom_call" | custom-call | flops 4831838208 | bytes 18880512 | tf_op jit(solution)/shard_map/back_feed/pallas_call | solution.py:288
  116.0 5.8 %grad_up.2 = (f32[384,768]{1,0:T(8,128)}, f32[384,768]{1,0:T(8,128)}) custom-call(s32[16]{0:T(128)} %get-tuple-element.222.from_ref, bf16[768,1024]{1,0:T(8,128)(2,1)} %get-tuple-element.152.refs_0_, bf16[1024,1536]{1,0:T(8,128)(2,1)} %get-tuple-element.153.refs_1_), custom_call_target="tpu_custom_call" | custom-call | flops 1207959552 | bytes 5505024 | tf_op jit(solution)/shard_map/grad_up/pallas_call | solution.py:396
  121.8 1.6 collective-permute-start.34
  123.4 6.0 %grad_up.3 = (f32[384,768]{1,0:T(8,128)}, f32[384,768]{1,0:T(8,128)}) custom-call(s32[16]{0:T(128)} %get-tuple-element.221.from_ref, bf16[768,1024]{1,0:T(8,128)(2,1)} %get-tuple-element.152.refs_0_, bf16[1024,1536]{1,0:T(8,128)(2,1)} %get-tuple-element.153.refs_1_), custom_call_target="tpu_custom_call" | custom-call | flops 1207959552 | bytes 5505024 | tf_op jit(solution)/shard_map/grad_up/pallas_call | solution.py:396
  129.9 1.8 slice_add_fusion.3
  133.3 17.8 %collective-permute-done.34 = f32[384,768]{1,0:T(8,128)} collective-permute-done((f32[384,768]{1,0:T(8,128)}, f32[384,768]{1,0:T(8,128)}, u32[]{:S(2)}, u32[]{:S(2)}) %collective-permute-start.34) | collective-permute-done | bytes 1179680 | tf_op jit(solution)/shard_map/ppermute | solution.py:315
  153.3 19.7 %collective-permute-done.38 = f32[384,768]{1,0:T(8,128)S(1)} collective-permute-done((f32[384,768]{1,0:T(8,128)}, f32[384,768]{1,0:T(8,128)S(1)}, u32[]{:S(2)}, u32[]{:S(2)}) %collective-permute-start.38) | collective-permute-done | bytes 1179680 | tf_op jit(solution)/shard_map/ppermute | solution.py:315
  173.3 1.5 collective-permute-start.44
  175.6 2.1 collective-permute-start.36
  177.7 5.4 %collective-permute-done.39 = f32[192,768]{1,0:T(8,128)S(1)} collective-permute-done((f32[192,768]{1,0:T(8,128)S(1)}, f32[192,768]{1,0:T(8,128)S(1)}, u32[]{:S(2)}, u32[]{:S(2)}) %collective-permute-start.39) | collective-permute-done | bytes 589856 | tf_op jit(solution)/shard_map/ppermute | solution.py:315
  183.2 2.1 collective-permute-start.40
  185.2 2.7 collective-permute-start.45
  188.4 2.7 collective-permute-start.49
  191.5 2.7 collective-permute-start.41
  194.3 5.3 %collective-permute-done.45 = f32[48,768]{1,0:T(8,128)S(1)} collective-permute-done((f32[48,768]{1,0:T(8,128)S(1)}, f32[48,768]{1,0:T(8,128)S(1)}, u32[]{:S(2)}, u32[]{:S(2)}) %collective-permute-start.45) | collective-permute-done | bytes 147488 | tf_op jit(solution)/shard_map/ppermute | solution.py:315
  199.6 1.5 collective-permute-done.49
  201.1 1.5 collective-permute-done.37
  205.0 1.7 copy-done.2
  206.7 9.2 %back_mid.1 = (f32[1024,768]{1,0:T(8,128)}, bf16[768,1024]{1,0:T(8,128)(2,1)}, bf16[1024,384]{1,0:T(8,128)(2,1)}, f32[1,768]{1,0:T(1,128)}, f32[1,768]{1,0:T(1,128)}, /*index=5*/f32[1,768]{1,0:T(1,128)}) custom-call(f32[1024,768]{1,0:T(8,128)} %get-tuple-element.101.mid_ref, f32[1024,768]{1,0:T(8,128)} %get-tuple-element.111.own_ref, f32[1024,768]{1,0:T(8,128)} %copy-done.2, ...), custom_call_target="tpu_custom_call" | custom-call | flops 603979776 | bytes 18690048 | tf_op jit(solution)/shard_map/back_mid/pallas_call | solution.py:288
  215.9 8.8 %back_attend.3 = (bf16[1024,128]{1,0:T(8,128)(2,1)}, bf16[1024,128]{1,0:T(8,128)(2,1)}, bf16[1024,128]{1,0:T(8,128)(2,1)}, f32[1,128]{1,0:T(1,128)}, f32[1,128]{1,0:T(1,128)}) custom-call(bf16[1024,384]{1,0:T(8,128)(2,1)} %get-tuple-element.90.q_ref, bf16[1024,384]{1,0:T(8,128)(2,1)} %get-tuple-element.91.k_ref, bf16[1024,384]{1,0:T(8,128)(2,1)} %get-tuple-element.92.v_ref, ...), custom_call_target="tpu_custom_call" | custom-call | flops 5368709120 | bytes 4752384 | tf_op jit(solution)/shard_map/back_attend/pallas_call | solution.py:288
  224.7 8.6 %back_attend.4 = (bf16[1024,128]{1,0:T(8,128)(2,1)}, bf16[1024,128]{1,0:T(8,128)(2,1)}, bf16[1024,128]{1,0:T(8,128)(2,1)}, f32[1,128]{1,0:T(1,128)}, f32[1,128]{1,0:T(1,128)}) custom-call(bf16[1024,384]{1,0:T(8,128)(2,1)} %get-tuple-element.90.q_ref, bf16[1024,384]{1,0:T(8,128)(2,1)} %get-tuple-element.91.k_ref, bf16[1024,384]{1,0:T(8,128)(2,1)} %get-tuple-element.92.v_ref, ...), custom_call_target="tpu_custom_call" | custom-call | flops 5368709120 | bytes 4752384 | tf_op jit(solution)/shard_map/back_attend/pallas_call | solution.py:288
  233.2 8.6 %back_attend.5 = (bf16[1024,128]{1,0:T(8,128)(2,1)}, bf16[1024,128]{1,0:T(8,128)(2,1)}, bf16[1024,128]{1,0:T(8,128)(2,1)}, f32[1,128]{1,0:T(1,128)}, f32[1,128]{1,0:T(1,128)}) custom-call(bf16[1024,384]{1,0:T(8,128)(2,1)} %get-tuple-element.90.q_ref, bf16[1024,384]{1,0:T(8,128)(2,1)} %get-tuple-element.91.k_ref, bf16[1024,384]{1,0:T(8,128)(2,1)} %get-tuple-element.92.v_ref, ...), custom_call_target="tpu_custom_call" | custom-call | flops 5368709120 | bytes 4752384 | tf_op jit(solution)/shard_map/back_attend/pallas_call | solution.py:288
  241.9 5.2 %grad_out.1 = (f32[384,384]{1,0:T(8,128)}, f32[384,384]{1,0:T(8,128)}) custom-call(s32[16]{0:T(128)} %broadcast_xor_fusion.2.from_ref, bf16[768,1024]{1,0:T(8,128)(2,1)} %get-tuple-element.143.refs_0_, bf16[1024,384]{1,0:T(8,128)(2,1)} %get-tuple-element.114.o_ref.refs_1_), custom_call_target="tpu_custom_call" | custom-call | flops 603979776 | bytes 3538944 | tf_op jit(solution)/shard_map/grad_out/pallas_call | solution.py:396
  249.3 4.4 %grad_qkv.3 = (f32[384,384]{1,0:T(8,128)}, f32[384,384]{1,0:T(8,128)}) custom-call(s32[16]{0:T(128)} %broadcast_xor_fusion.3.from_ref, bf16[768,1024]{1,0:T(8,128)(2,1)} %get-tuple-element.136.refs_0_, bf16[1024,128]{1,0:T(8,128)(2,1)} %get-tuple-element.116.refs_0_.refs_1_, bf16[1024,128]{1,0:T(8,128)(2,1)} %get-tuple-element.117.refs_1_.refs_2_, ...), custom_call_target="tpu_custom_call" | custom-call | flops 603979776 | bytes 3538944 | tf_op jit(solution)/shard_map/grad_qkv/pallas_call | solution.py:396
  255.1 2.3 collective-permute-done.30
  258.9 6.5 %back_project.1.own_ref = f32[1024,768]{1,0:T(8,128)} custom-call(bf16[1024,128]{1,0:T(8,128)(2,1)} %get-tuple-element.116.refs_0_.refs_1_, bf16[1024,128]{1,0:T(8,128)(2,1)} %get-tuple-element.117.refs_1_.refs_2_, bf16[1024,128]{1,0:T(8,128)(2,1)} %get-tuple-element.118.refs_2_.refs_3_, bf16[1024,128]{1,0:T(8,128)(2,1)} %get-tuple-element.119.refs_3_.refs_1_, ...), custom_call_target="tpu_custom_call" | custom-call | flops 1811939328 | bytes 7274496 | tf_op jit(solution)/shard_map/back_project/pallas_call | solution.py:288
  265.9 4.6 %grad_qkv.4 = (f32[384,384]{1,0:T(8,128)}, f32[384,384]{1,0:T(8,128)}) custom-call(s32[16]{0:T(128)} %broadcast_xor_fusion.2.from_ref, bf16[768,1024]{1,0:T(8,128)(2,1)} %get-tuple-element.136.refs_0_, bf16[1024,128]{1,0:T(8,128)(2,1)} %get-tuple-element.119.refs_3_.refs_1_, bf16[1024,128]{1,0:T(8,128)(2,1)} %get-tuple-element.120.refs_4_.refs_2_, ...), custom_call_target="tpu_custom_call" | custom-call | flops 603979776 | bytes 3538944 | tf_op jit(solution)/shard_map/grad_qkv/pallas_call | solution.py:396
  270.5 3.4 %collective-permute-start.33 = (f32[1,4608]{1,0:T(1,128)S(1)}, f32[1,4608]{1,0:T(1,128)S(1)}, u32[]{:S(2)}, u32[]{:S(2)}) collective-permute-start(f32[1,4608]{1,0:T(1,128)S(1)} %add.254), channel_id=1, source_target_pairs={{0,16},{2,18},{4,20},{6,22},{8,24},{10,26},{12,28},{14,30},{16,0},... | collective-permute-start | bytes 55304 | tf_op jit(solution)/shard_map/ppermute | solution.py:315
  273.9 4.3 %grad_qkv.5 = (f32[384,384]{1,0:T(8,128)}, f32[384,384]{1,0:T(8,128)}) custom-call(s32[16]{0:T(128)} %broadcast_xor_fusion.3.from_ref, bf16[768,1024]{1,0:T(8,128)(2,1)} %get-tuple-element.136.refs_0_, bf16[1024,128]{1,0:T(8,128)(2,1)} %get-tuple-element.122.refs_6_.refs_1_, bf16[1024,128]{1,0:T(8,128)(2,1)} %get-tuple-element.123.refs_7_.refs_2_, ...), custom_call_target="tpu_custom_call" | custom-call | flops 603979776 | bytes 3538944 | tf_op jit(solution)/shard_map/grad_qkv/pallas_call | solution.py:396
  278.5 2.0 collective-permute-start.22
  283.2 1.8 collective-permute-start.15
  285.0 5.2 %collective-permute-done.18 = f32[384,384]{1,0:T(8,128)S(1)} collective-permute-done((f32[384,384]{1,0:T(8,128)}, f32[384,384]{1,0:T(8,128)S(1)}, u32[]{:S(2)}, u32[]{:S(2)}) %collective-permute-start.18) | collective-permute-done | bytes 589856 | tf_op jit(solution)/shard_map/ppermute | solution.py:315
  290.3 2.4 collective-permute-start.19
  293.6 1.8 collective-permute-start.23
  295.4 2.7 collective-permute-done.27
  298.2 2.1 collective-permute-start.16
  301.4 2.1 collective-permute-start.24
  303.5 3.5 %collective-permute-done.28 = f32[96,384]{1,0:T(8,128)S(1)} collective-permute-done((f32[96,384]{1,0:T(8,128)S(1)}, f32[96,384]{1,0:T(8,128)S(1)}, u32[]{:S(2)}, u32[]{:S(2)}) %collective-permute-start.28) | collective-permute-done | bytes 147488 | tf_op jit(solution)/shard_map/ppermute | solution.py:315
  307.0 2.2 collective-permute-done.16
  315.5 1.8 copy-done.3
  317.3 7.3 %back_input.1 = (f32[1024,768]{1,0:T(8,128)}, f32[1,768]{1,0:T(1,128)}, f32[1,768]{1,0:T(1,128)}, f32[1,768]{1,0:T(1,128)}) custom-call(bf16[1024,768]{1,0:T(8,128)(2,1)} %bitcast.14, f32[1,768]{1,0:T(1,128)} %time_ref.7, f32[1024,768]{1,0:T(8,128)} %back_project.1.own_ref, f32[1024,768]{1,0:T(8,128)} %copy-done.3, f32[1024,768]{1,0:T(8,128)} %get-tuple-element.125.mg_ref, ...), custom_call_target="tpu_custom_call" | custom-call | bytes 14171136 | tf_op jit(solution)/shard_map/back_input/pallas_call | solution.py:288
  326.1 1.7 collective-permute-start.10
  327.8 2.0 collective-permute-done.10
  330.4 3.1 collective-permute-done.11
  333.8 3.5 %collective-permute-done.12 = f32[1,2304]{1,0:T(1,128)S(1)} collective-permute-done((f32[1,2304]{1,0:T(1,128)S(1)}, f32[1,2304]{1,0:T(1,128)S(1)}, u32[]{:S(2)}, u32[]{:S(2)}) %collective-permute-start.12) | collective-permute-done | bytes 9248 | tf_op jit(solution)/shard_map/ppermute | solution.py:315
  337.3 1.7 collective-permute-start.13
  339.8 2.1 collective-permute-done.13
  (209 shorter events, 45.2 us)
Async XLA Ops:
  21.8 15.0 %collective-permute-start.1 = (f32[512,768]{1,0:T(8,128)}, f32[512,768]{1,0:T(8,128)S(1)}, u32[]{:S(2)}, u32[]{:S(2)}) collective-permute-start(f32[512,768]{1,0:T(8,128)} %get-tuple-element.96.own_ref), channel_id=1, source_target_pairs={{0,1},{1,0},{2,3},{3,2},{4,5},{5,4},{6,7},{7,6},{8,9},{9,8},{10,11... | collective-permute-start | bytes 4718600 | tf_op jit(solution)/shard_map/ppermute | solution.py:303
  22.2 12.1 %copy-start.17 = (f32[768]{0:T(1024)S(1)}, f32[768]{0:T(1024)}, u32[]{:S(2)}) copy-start(f32[768]{0:T(1024)} %param.34) | copy-start | bytes 9220
  22.2 12.7 %copy-start.15 = (f32[1536]{0:T(1024)S(1)}, f32[1536]{0:T(1024)}, u32[]{:S(2)}) copy-start(f32[1536]{0:T(1024)} %param.37) | copy-start | bytes 18436
  22.2 13.3 %copy-start.18 = (f32[768]{0:T(1024)S(1)}, f32[768]{0:T(1024)}, u32[]{:S(2)}) copy-start(f32[768]{0:T(1024)} %param.33) | copy-start | bytes 9220
  22.2 13.9 %copy-start.19 = (f32[768]{0:T(1024)S(1)}, f32[768]{0:T(1024)}, u32[]{:S(2)}) copy-start(f32[768]{0:T(1024)} %param.35) | copy-start | bytes 9220
  34.3 13.9 %collective-permute-start = (f32[512,768]{1,0:T(8,128)}, f32[512,768]{1,0:T(8,128)S(1)}, u32[]{:S(2)}, u32[]{:S(2)}) collective-permute-start(f32[512,768]{1,0:T(8,128)} %get-tuple-element.95.own_ref), channel_id=1, source_target_pairs={{0,1},{1,0},{2,3},{3,2},{4,5},{5,4},{6,7},{7,6},{8,9},{9,8},{10,11... | collective-permute-start | bytes 4718600 | tf_op jit(solution)/shard_map/ppermute | solution.py:303
  47.7 30.9 %collective-permute-start.7 = (f32[512,768]{1,0:T(8,128)}, f32[512,768]{1,0:T(8,128)S(1)}, u32[]{:S(2)}, u32[]{:S(2)}) collective-permute-start(f32[512,768]{1,0:T(8,128)} %get-tuple-element.103.own_ref), channel_id=1, source_target_pairs={{0,1},{1,0},{2,3},{3,2},{4,5},{5,4},{6,7},{7,6},{8,9},{9,8},{10,11... | collective-permute-start | bytes 4718600 | tf_op jit(solution)/shard_map/ppermute | solution.py:303
  49.4 13.7 %copy-start.20 = (f32[768]{0:T(1024)S(1)}, f32[768]{0:T(1024)}, u32[]{:S(2)}) copy-start(f32[768]{0:T(1024)} %param.39) | copy-start | bytes 9220
  49.4 14.2 %copy-start.29 = (s32[16]{0:T(128)S(1)}, s32[16]{0:T(128)}, u32[]{:S(2)}) copy-start(s32[16]{0:T(128)} %constant.31.clone) | copy-start | bytes 196
  49.4 14.8 %copy-start.28 = (s32[16]{0:T(128)S(1)}, s32[16]{0:T(128)}, u32[]{:S(2)}) copy-start(s32[16]{0:T(128)} %constant.32.clone) | copy-start | bytes 196
  49.4 15.3 %copy-start.26 = (s32[16]{0:T(128)S(1)}, s32[16]{0:T(128)}, u32[]{:S(2)}) copy-start(s32[16]{0:T(128)} %constant.33.clone) | copy-start | bytes 196
  49.4 15.3 %copy-start.27 = (s32[16]{0:T(128)S(1)}, s32[16]{0:T(128)}, u32[]{:S(2)}) copy-start(s32[16]{0:T(128)} %constant.34.clone) | copy-start | bytes 196
  59.3 24.7 %collective-permute-start.2 = (f32[512,768]{1,0:T(8,128)}, f32[512,768]{1,0:T(8,128)S(1)}, u32[]{:S(2)}, u32[]{:S(2)}) collective-permute-start(f32[512,768]{1,0:T(8,128)} %get-tuple-element.102.own_ref), channel_id=1, source_target_pairs={{0,1},{1,0},{2,3},{3,2},{4,5},{5,4},{6,7},{7,6},{8,9},{9,8},{10,11... | collective-permute-start | bytes 4718600 | tf_op jit(solution)/shard_map/ppermute | solution.py:303
  60.1 5.2 %collective-permute-start.3 = (s32[4]{0:T(128)S(1)}, s32[4]{0:T(128)S(1)}, u32[]{:S(2)}, u32[]{:S(2)}) collective-permute-start(s32[4]{0:T(128)S(1)} %compare_convert_fusion), channel_id=1, source_target_pairs={{0,2},{2,0},{4,6},{6,4},{8,10},{10,8},{12,14},{14,12},{16,18},{18,... | collective-permute-start | bytes 56 | tf_op jit(solution)/shard_map/ppermute | solution.py:315
  65.2 3.6 %collective-permute-start.4 = (s32[4]{0:T(128)S(1)}, s32[4]{0:T(128)S(1)}, u32[]{:S(2)}, u32[]{:S(2)}) collective-permute-start(s32[4]{0:T(128)S(1)} %fusion.10), channel_id=1, source_target_pairs={{0,4},{2,6},{4,0},{6,2},{8,12},{10,14},{12,8},{14,10},{16,20},{18,... | collective-permute-start | bytes 56 | tf_op jit(solution)/shard_map/ppermute | solution.py:315
  68.8 3.5 %collective-permute-start.5 = (s32[4]{0:T(128)S(1)}, s32[4]{0:T(128)S(1)}, u32[]{:S(2)}, u32[]{:S(2)}) collective-permute-start(s32[4]{0:T(128)S(1)} %fusion.11), channel_id=1, source_target_pairs={{0,8},{2,10},{4,12},{6,14},{8,0},{10,2},{12,4},{14,6},{16,24},{18,... | collective-permute-start | bytes 56 | tf_op jit(solution)/shard_map/ppermute | solution.py:315
  72.4 4.4 %collective-permute-start.6 = (s32[4]{0:T(128)S(1)}, s32[4]{0:T(128)S(1)}, u32[]{:S(2)}, u32[]{:S(2)}) collective-permute-start(s32[4]{0:T(128)S(1)} %add.217), channel_id=1, source_target_pairs={{0,16},{2,18},{4,20},{6,22},{8,24},{10,26},{12,28},{14,30},{16,0},... | collective-permute-start | bytes 56 | tf_op jit(solution)/shard_map/ppermute | solution.py:315
  95.1 34.8 %collective-permute-start.42 = (f32[384,768]{1,0:T(8,128)}, f32[384,768]{1,0:T(8,128)}, u32[]{:S(2)}, u32[]{:S(2)}) collective-permute-start(f32[384,768]{1,0:T(8,128)} %get-tuple-element.161), channel_id=1, source_target_pairs={{0,2},{2,0},{4,6},{6,4},{8,10},{10,8},{12,14},{14,12},{16,18},{18,... | collective-permute-start | bytes 3538952 | tf_op jit(solution)/shard_map/ppermute | solution.py:315
  102.2 30.1 %collective-permute-start.46 = (f32[384,768]{1,0:T(8,128)}, f32[384,768]{1,0:T(8,128)S(1)}, u32[]{:S(2)}, u32[]{:S(2)}) collective-permute-start(f32[384,768]{1,0:T(8,128)} %get-tuple-element.163), channel_id=1, source_target_pairs={{0,4},{2,6},{4,0},{6,2},{8,12},{10,14},{12,8},{14,10},{16,20},{18,... | collective-permute-start | bytes 3538952 | tf_op jit(solution)/shard_map/ppermute | solution.py:315
  121.8 29.2 %collective-permute-start.34 = (f32[384,768]{1,0:T(8,128)}, f32[384,768]{1,0:T(8,128)}, u32[]{:S(2)}, u32[]{:S(2)}) collective-permute-start(f32[384,768]{1,0:T(8,128)} %get-tuple-element.155), channel_id=1, source_target_pairs={{0,8},{2,10},{4,12},{6,14},{8,0},{10,2},{12,4},{14,6},{16,24},{18,... | collective-permute-start | bytes 3538952 | tf_op jit(solution)/shard_map/ppermute | solution.py:315
  129.4 43.6 %collective-permute-start.38 = (f32[384,768]{1,0:T(8,128)}, f32[384,768]{1,0:T(8,128)S(1)}, u32[]{:S(2)}, u32[]{:S(2)}) collective-permute-start(f32[384,768]{1,0:T(8,128)} %get-tuple-element.157), channel_id=1, source_target_pairs={{0,8},{2,10},{4,12},{6,14},{8,0},{10,2},{12,4},{14,6},{16,24},{18,... | collective-permute-start | bytes 3538952 | tf_op jit(solution)/shard_map/ppermute | solution.py:315
  129.9 75.2 %collective-permute-start.8 = (f32[1024,768]{1,0:T(8,128)S(1)}, f32[1024,768]{1,0:T(8,128)S(1)}, u32[]{:S(2)}, u32[]{:S(2)}) collective-permute-start(f32[1024,768]{1,0:T(8,128)S(1)} %copy-done.1), channel_id=1, source_target_pairs={{0,1},{1,0},{2,3},{3,2},{4,5},{5,4},{6,7},{7,6},{8,9},{9,8},{10,11... | collective-permute-start | bytes 9437192 | tf_op jit(solution)/shard_map/ppermute | solution.py:303
  131.7 41.5 %collective-permute-start.43 = (f32[192,768]{1,0:T(8,128)S(1)}, f32[192,768]{1,0:T(8,128)S(1)}, u32[]{:S(2)}, u32[]{:S(2)}) collective-permute-start(f32[192,768]{1,0:T(8,128)S(1)} %get-tuple-element.190), channel_id=1, source_target_pairs={{0,4},{2,6},{4,0},{6,2},{8,12},{10,14},{12,8},{14,10},{16,20},{18,... | collective-permute-start | bytes 1769480 | tf_op jit(solution)/shard_map/ppermute | solution.py:315
  132.3 18.7 %copy-start.10 = (f32[384,768]{1,0:T(8,128)S(1)}, f32[384,768]{1,0:T(8,128)}, u32[]{:S(2)}) copy-start(f32[384,768]{1,0:T(8,128)} %get-tuple-element.154) | copy-start | bytes 3538948
  132.5 42.4 %collective-permute-start.47 = (f32[192,768]{1,0:T(8,128)S(1)}, f32[192,768]{1,0:T(8,128)S(1)}, u32[]{:S(2)}, u32[]{:S(2)}) collective-permute-start(f32[192,768]{1,0:T(8,128)S(1)} %get-tuple-element.192), channel_id=1, source_target_pairs={{0,2},{2,0},{4,6},{6,4},{8,10},{10,8},{12,14},{14,12},{16,18},{18,... | collective-permute-start | bytes 1769480 | tf_op jit(solution)/shard_map/ppermute | solution.py:315
  151.1 21.9 %copy-start.8 = (f32[384,768]{1,0:T(8,128)S(1)}, f32[384,768]{1,0:T(8,128)}, u32[]{:S(2)}) copy-start(f32[384,768]{1,0:T(8,128)} %get-tuple-element.156) | copy-start | bytes 3538948
  152.6 23.0 %collective-permute-start.35 = (f32[192,768]{1,0:T(8,128)S(1)}, f32[192,768]{1,0:T(8,128)S(1)}, u32[]{:S(2)}, u32[]{:S(2)}) collective-permute-start(f32[192,768]{1,0:T(8,128)S(1)} %get-tuple-element.194), channel_id=1, source_target_pairs={{0,2},{2,0},{4,6},{6,4},{8,10},{10,8},{12,14},{14,12},{16,18},{18,... | collective-permute-start | bytes 1769480 | tf_op jit(solution)/shard_map/ppermute | solution.py:315
  173.2 9.9 %collective-permute-start.39 = (f32[192,768]{1,0:T(8,128)S(1)}, f32[192,768]{1,0:T(8,128)S(1)}, u32[]{:S(2)}, u32[]{:S(2)}) collective-permute-start(f32[192,768]{1,0:T(8,128)S(1)} %get-tuple-element.196), channel_id=1, source_target_pairs={{0,4},{2,6},{4,0},{6,2},{8,12},{10,14},{12,8},{14,10},{16,20},{18,... | collective-permute-start | bytes 1769480 | tf_op jit(solution)/shard_map/ppermute | solution.py:315
  173.3 11.9 %collective-permute-start.44 = (f32[96,768]{1,0:T(8,128)S(1)}, f32[96,768]{1,0:T(8,128)S(1)}, u32[]{:S(2)}, u32[]{:S(2)}) collective-permute-start(f32[96,768]{1,0:T(8,128)S(1)} %get-tuple-element.198), channel_id=1, source_target_pairs={{0,8},{2,10},{4,12},{6,14},{8,0},{10,2},{12,4},{14,6},{16,24},{18,... | collective-permute-start | bytes 884744 | tf_op jit(solution)/shard_map/ppermute | solution.py:315
  174.9 13.5 %collective-permute-start.48 = (f32[96,768]{1,0:T(8,128)S(1)}, f32[96,768]{1,0:T(8,128)S(1)}, u32[]{:S(2)}, u32[]{:S(2)}) collective-permute-start(f32[96,768]{1,0:T(8,128)S(1)} %get-tuple-element.200), channel_id=1, source_target_pairs={{0,8},{2,10},{4,12},{6,14},{8,0},{10,2},{12,4},{14,6},{16,24},{18,... | collective-permute-start | bytes 884744 | tf_op jit(solution)/shard_map/ppermute | solution.py:315
  175.6 15.5 %collective-permute-start.36 = (f32[96,768]{1,0:T(8,128)S(1)}, f32[96,768]{1,0:T(8,128)S(1)}, u32[]{:S(2)}, u32[]{:S(2)}) collective-permute-start(f32[96,768]{1,0:T(8,128)S(1)} %get-tuple-element.202), channel_id=1, source_target_pairs={{0,4},{2,6},{4,0},{6,2},{8,12},{10,14},{12,8},{14,10},{16,20},{18,... | collective-permute-start | bytes 884744 | tf_op jit(solution)/shard_map/ppermute | solution.py:315
  183.2 8.4 %collective-permute-start.40 = (f32[96,768]{1,0:T(8,128)S(1)}, f32[96,768]{1,0:T(8,128)S(1)}, u32[]{:S(2)}, u32[]{:S(2)}) collective-permute-start(f32[96,768]{1,0:T(8,128)S(1)} %get-tuple-element.204), channel_id=1, source_target_pairs={{0,2},{2,0},{4,6},{6,4},{8,10},{10,8},{12,14},{14,12},{16,18},{18,... | collective-permute-start | bytes 884744 | tf_op jit(solution)/shard_map/ppermute | solution.py:315
  185.2 14.3 %collective-permute-start.45 = (f32[48,768]{1,0:T(8,128)S(1)}, f32[48,768]{1,0:T(8,128)S(1)}, u32[]{:S(2)}, u32[]{:S(2)}) collective-permute-start(f32[48,768]{1,0:T(8,128)S(1)} %slice_add_fusion.26), channel_id=1, source_target_pairs={{0,16},{2,18},{4,20},{6,22},{8,24},{10,26},{12,28},{14,30},{16,0},... | collective-permute-start | bytes 442376 | tf_op jit(solution)/shard_map/ppermute | solution.py:315
  188.4 12.7 %collective-permute-start.49 = (f32[48,768]{1,0:T(8,128)S(1)}, f32[48,768]{1,0:T(8,128)S(1)}, u32[]{:S(2)}, u32[]{:S(2)}) collective-permute-start(f32[48,768]{1,0:T(8,128)S(1)} %slice_add_fusion.24), channel_id=1, source_target_pairs={{0,16},{2,18},{4,20},{6,22},{8,24},{10,26},{12,28},{14,30},{16,0},... | collective-permute-start | bytes 442376 | tf_op jit(solution)/shard_map/ppermute | solution.py:315
  191.2 11.5 %collective-permute-start.37 = (f32[48,768]{1,0:T(8,128)S(1)}, f32[48,768]{1,0:T(8,128)S(1)}, u32[]{:S(2)}, u32[]{:S(2)}) collective-permute-start(f32[48,768]{1,0:T(8,128)S(1)} %slice_add_fusion.30), channel_id=1, source_target_pairs={{0,16},{2,18},{4,20},{6,22},{8,24},{10,26},{12,28},{14,30},{16,0},... | collective-permute-start | bytes 442376 | tf_op jit(solution)/shard_map/ppermute | solution.py:315
  191.5 12.7 %collective-permute-start.41 = (f32[48,768]{1,0:T(8,128)S(1)}, f32[48,768]{1,0:T(8,128)S(1)}, u32[]{:S(2)}, u32[]{:S(2)}) collective-permute-start(f32[48,768]{1,0:T(8,128)S(1)} %slice_add_fusion.28), channel_id=1, source_target_pairs={{0,16},{2,18},{4,20},{6,22},{8,24},{10,26},{12,28},{14,30},{16,0},... | collective-permute-start | bytes 442376 | tf_op jit(solution)/shard_map/ppermute | solution.py:315
  247.1 34.7 %collective-permute-start.26 = (f32[384,384]{1,0:T(8,128)}, f32[384,384]{1,0:T(8,128)S(1)}, u32[]{:S(2)}, u32[]{:S(2)}) collective-permute-start(f32[384,384]{1,0:T(8,128)} %get-tuple-element.145), channel_id=1, source_target_pairs={{0,2},{2,0},{4,6},{6,4},{8,10},{10,8},{12,14},{14,12},{16,18},{18,... | collective-permute-start | bytes 1769480 | tf_op jit(solution)/shard_map/ppermute | solution.py:315
  247.8 9.6 %collective-permute-start.30 = (f32[1,4608]{1,0:T(1,128)S(1)}, f32[1,4608]{1,0:T(1,128)S(1)}, u32[]{:S(2)}, u32[]{:S(2)}) collective-permute-start(f32[1,4608]{1,0:T(1,128)S(1)} %constant_dynamic-update-slice_fusion.8), channel_id=1, source_target_pairs={{0,2},{2,0},{4,6},{6,4},{8,10},{10,8},{12,14},{14,12},{16,18},{18,... | collective-permute-start | bytes 55304 | tf_op jit(solution)/shard_map/ppermute | solution.py:315
  253.7 28.3 %collective-permute-start.14 = (f32[384,384]{1,0:T(8,128)}, f32[384,384]{1,0:T(8,128)}, u32[]{:S(2)}, u32[]{:S(2)}) collective-permute-start(f32[384,384]{1,0:T(8,128)} %get-tuple-element.138), channel_id=1, source_target_pairs={{0,4},{2,6},{4,0},{6,2},{8,12},{10,14},{12,8},{14,10},{16,20},{18,... | collective-permute-start | bytes 1769480 | tf_op jit(solution)/shard_map/ppermute | solution.py:315
  257.4 8.0 %collective-permute-start.31 = (f32[1,4608]{1,0:T(1,128)S(1)}, f32[1,4608]{1,0:T(1,128)S(1)}, u32[]{:S(2)}, u32[]{:S(2)}) collective-permute-start(f32[1,4608]{1,0:T(1,128)S(1)} %add.252), channel_id=1, source_target_pairs={{0,4},{2,6},{4,0},{6,2},{8,12},{10,14},{12,8},{14,10},{16,20},{18,... | collective-permute-start | bytes 55304 | tf_op jit(solution)/shard_map/ppermute | solution.py:315
  265.5 5.0 %collective-permute-start.32 = (f32[1,4608]{1,0:T(1,128)S(1)}, f32[1,4608]{1,0:T(1,128)S(1)}, u32[]{:S(2)}, u32[]{:S(2)}) collective-permute-start(f32[1,4608]{1,0:T(1,128)S(1)} %add.253), channel_id=1, source_target_pairs={{0,8},{2,10},{4,12},{6,14},{8,0},{10,2},{12,4},{14,6},{16,24},{18,... | collective-permute-start | bytes 55304 | tf_op jit(solution)/shard_map/ppermute | solution.py:315
  265.9 14.6 %copy-start = (f32[1024,768]{1,0:T(8,128)S(1)}, f32[1024,768]{1,0:T(8,128)}, u32[]{:S(2)}) copy-start(f32[1024,768]{1,0:T(8,128)} %back_project.1.own_ref) | copy-start | bytes 9437188
  270.5 11.5 %copy-start.12 = (f32[384,384]{1,0:T(8,128)S(1)}, f32[384,384]{1,0:T(8,128)}, u32[]{:S(2)}) copy-start(f32[384,384]{1,0:T(8,128)} %get-tuple-element.137) | copy-start | bytes 1769476
  270.5 10.0 %collective-permute-start.33 = (f32[1,4608]{1,0:T(1,128)S(1)}, f32[1,4608]{1,0:T(1,128)S(1)}, u32[]{:S(2)}, u32[]{:S(2)}) collective-permute-start(f32[1,4608]{1,0:T(1,128)S(1)} %add.254), channel_id=1, source_target_pairs={{0,16},{2,18},{4,20},{6,22},{8,24},{10,26},{12,28},{14,30},{16,0},... | collective-permute-start | bytes 55304 | tf_op jit(solution)/shard_map/ppermute | solution.py:315
  278.2 12.0 %collective-permute-start.18 = (f32[384,384]{1,0:T(8,128)}, f32[384,384]{1,0:T(8,128)S(1)}, u32[]{:S(2)}, u32[]{:S(2)}) collective-permute-start(f32[384,384]{1,0:T(8,128)} %get-tuple-element.140), channel_id=1, source_target_pairs={{0,2},{2,0},{4,6},{6,4},{8,10},{10,8},{12,14},{14,12},{16,18},{18,... | collective-permute-start | bytes 1769480 | tf_op jit(solution)/shard_map/ppermute | solution.py:315
  278.5 15.0 %collective-permute-start.22 = (f32[384,384]{1,0:T(8,128)}, f32[384,384]{1,0:T(8,128)S(1)}, u32[]{:S(2)}, u32[]{:S(2)}) collective-permute-start(f32[384,384]{1,0:T(8,128)} %get-tuple-element.142), channel_id=1, source_target_pairs={{0,4},{2,6},{4,0},{6,2},{8,12},{10,14},{12,8},{14,10},{16,20},{18,... | collective-permute-start | bytes 1769480 | tf_op jit(solution)/shard_map/ppermute | solution.py:315
  280.5 35.0 %collective-permute-start.9 = (f32[1024,768]{1,0:T(8,128)S(1)}, f32[1024,768]{1,0:T(8,128)S(1)}, u32[]{:S(2)}, u32[]{:S(2)}) collective-permute-start(f32[1024,768]{1,0:T(8,128)S(1)} %copy-done), channel_id=1, source_target_pairs={{0,1},{1,0},{2,3},{3,2},{4,5},{5,4},{6,7},{7,6},{8,9},{9,8},{10,11... | collective-permute-start | bytes 9437192 | tf_op jit(solution)/shard_map/ppermute | solution.py:303
  281.8 16.2 %collective-permute-start.27 = (f32[192,384]{1,0:T(8,128)S(1)}, f32[192,384]{1,0:T(8,128)S(1)}, u32[]{:S(2)}, u32[]{:S(2)}) collective-permute-start(f32[192,384]{1,0:T(8,128)S(1)} %get-tuple-element.206), channel_id=1, source_target_pairs={{0,4},{2,6},{4,0},{6,2},{8,12},{10,14},{12,8},{14,10},{16,20},{18,... | collective-permute-start | bytes 884744 | tf_op jit(solution)/shard_map/ppermute | solution.py:315
  282.0 11.5 %copy-start.14 = (f32[384,384]{1,0:T(8,128)S(1)}, f32[384,384]{1,0:T(8,128)}, u32[]{:S(2)}) copy-start(f32[384,384]{1,0:T(8,128)} %get-tuple-element.141) | copy-start | bytes 1769476
  283.2 15.0 %collective-permute-start.15 = (f32[192,384]{1,0:T(8,128)S(1)}, f32[192,384]{1,0:T(8,128)S(1)}, u32[]{:S(2)}, u32[]{:S(2)}) collective-permute-start(f32[192,384]{1,0:T(8,128)S(1)} %get-tuple-element.208), channel_id=1, source_target_pairs={{0,2},{2,0},{4,6},{6,4},{8,10},{10,8},{12,14},{14,12},{16,18},{18,... | collective-permute-start | bytes 884744 | tf_op jit(solution)/shard_map/ppermute | solution.py:315
  290.3 10.9 %collective-permute-start.19 = (f32[192,384]{1,0:T(8,128)S(1)}, f32[192,384]{1,0:T(8,128)S(1)}, u32[]{:S(2)}, u32[]{:S(2)}) collective-permute-start(f32[192,384]{1,0:T(8,128)S(1)} %get-tuple-element.210), channel_id=1, source_target_pairs={{0,4},{2,6},{4,0},{6,2},{8,12},{10,14},{12,8},{14,10},{16,20},{18,... | collective-permute-start | bytes 884744 | tf_op jit(solution)/shard_map/ppermute | solution.py:315
  293.6 7.8 %collective-permute-start.23 = (f32[192,384]{1,0:T(8,128)S(1)}, f32[192,384]{1,0:T(8,128)S(1)}, u32[]{:S(2)}, u32[]{:S(2)}) collective-permute-start(f32[192,384]{1,0:T(8,128)S(1)} %get-tuple-element.212), channel_id=1, source_target_pairs={{0,2},{2,0},{4,6},{6,4},{8,10},{10,8},{12,14},{14,12},{16,18},{18,... | collective-permute-start | bytes 884744 | tf_op jit(solution)/shard_map/ppermute | solution.py:315
  298.1 8.8 %collective-permute-start.28 = (f32[96,384]{1,0:T(8,128)S(1)}, f32[96,384]{1,0:T(8,128)S(1)}, u32[]{:S(2)}, u32[]{:S(2)}) collective-permute-start(f32[96,384]{1,0:T(8,128)S(1)} %get-tuple-element.214), channel_id=1, source_target_pairs={{0,8},{2,10},{4,12},{6,14},{8,0},{10,2},{12,4},{14,6},{16,24},{18,... | collective-permute-start | bytes 442376 | tf_op jit(solution)/shard_map/ppermute | solution.py:315
  298.2 11.0 %collective-permute-start.16 = (f32[96,384]{1,0:T(8,128)S(1)}, f32[96,384]{1,0:T(8,128)S(1)}, u32[]{:S(2)}, u32[]{:S(2)}) collective-permute-start(f32[96,384]{1,0:T(8,128)S(1)} %get-tuple-element.216), channel_id=1, source_target_pairs={{0,8},{2,10},{4,12},{6,14},{8,0},{10,2},{12,4},{14,6},{16,24},{18,... | collective-permute-start | bytes 442376 | tf_op jit(solution)/shard_map/ppermute | solution.py:315
  301.3 9.5 %collective-permute-start.20 = (f32[96,384]{1,0:T(8,128)S(1)}, f32[96,384]{1,0:T(8,128)S(1)}, u32[]{:S(2)}, u32[]{:S(2)}) collective-permute-start(f32[96,384]{1,0:T(8,128)S(1)} %get-tuple-element.218), channel_id=1, source_target_pairs={{0,8},{2,10},{4,12},{6,14},{8,0},{10,2},{12,4},{14,6},{16,24},{18,... | collective-permute-start | bytes 442376 | tf_op jit(solution)/shard_map/ppermute | solution.py:315
  301.4 12.1 %collective-permute-start.24 = (f32[96,384]{1,0:T(8,128)S(1)}, f32[96,384]{1,0:T(8,128)S(1)}, u32[]{:S(2)}, u32[]{:S(2)}) collective-permute-start(f32[96,384]{1,0:T(8,128)S(1)} %get-tuple-element.220), channel_id=1, source_target_pairs={{0,8},{2,10},{4,12},{6,14},{8,0},{10,2},{12,4},{14,6},{16,24},{18,... | collective-permute-start | bytes 442376 | tf_op jit(solution)/shard_map/ppermute | solution.py:315
  306.9 7.9 %collective-permute-start.29 = (f32[48,384]{1,0:T(8,128)S(1)}, f32[48,384]{1,0:T(8,128)S(1)}, u32[]{:S(2)}, u32[]{:S(2)}) collective-permute-start(f32[48,384]{1,0:T(8,128)S(1)} %slice_add_fusion.40), channel_id=1, source_target_pairs={{0,16},{2,18},{4,20},{6,22},{8,24},{10,26},{12,28},{14,30},{16,0},... | collective-permute-start | bytes 221192 | tf_op jit(solution)/shard_map/ppermute | solution.py:315
  309.2 18.6 %collective-permute-start.17 = (f32[48,384]{1,0:T(8,128)S(1)}, f32[48,384]{1,0:T(8,128)S(1)}, u32[]{:S(2)}, u32[]{:S(2)}) collective-permute-start(f32[48,384]{1,0:T(8,128)S(1)} %slice_add_fusion.46), channel_id=1, source_target_pairs={{0,16},{2,18},{4,20},{6,22},{8,24},{10,26},{12,28},{14,30},{16,0},... | collective-permute-start | bytes 221192 | tf_op jit(solution)/shard_map/ppermute | solution.py:315
  310.8 19.6 %collective-permute-start.21 = (f32[48,384]{1,0:T(8,128)S(1)}, f32[48,384]{1,0:T(8,128)S(1)}, u32[]{:S(2)}, u32[]{:S(2)}) collective-permute-start(f32[48,384]{1,0:T(8,128)S(1)} %slice_add_fusion.44), channel_id=1, source_target_pairs={{0,16},{2,18},{4,20},{6,22},{8,24},{10,26},{12,28},{14,30},{16,0},... | collective-permute-start | bytes 221192 | tf_op jit(solution)/shard_map/ppermute | solution.py:315
  313.5 20.2 %collective-permute-start.25 = (f32[48,384]{1,0:T(8,128)S(1)}, f32[48,384]{1,0:T(8,128)S(1)}, u32[]{:S(2)}, u32[]{:S(2)}) collective-permute-start(f32[48,384]{1,0:T(8,128)S(1)} %slice_add_fusion.42), channel_id=1, source_target_pairs={{0,16},{2,18},{4,20},{6,22},{8,24},{10,26},{12,28},{14,30},{16,0},... | collective-permute-start | bytes 221192 | tf_op jit(solution)/shard_map/ppermute | solution.py:315
  326.1 3.7 %collective-permute-start.10 = (f32[1,2304]{1,0:T(1,128)S(1)}, f32[1,2304]{1,0:T(1,128)S(1)}, u32[]{:S(2)}, u32[]{:S(2)}) collective-permute-start(f32[1,2304]{1,0:T(1,128)S(1)} %constant_dynamic-update-slice_fusion), channel_id=1, source_target_pairs={{0,2},{2,0},{4,6},{6,4},{8,10},{10,8},{12,14},{14,12},{16,18},{18,... | collective-permute-start | bytes 27656 | tf_op jit(solution)/shard_map/ppermute | solution.py:315
  329.8 3.7 %collective-permute-start.11 = (f32[1,2304]{1,0:T(1,128)S(1)}, f32[1,2304]{1,0:T(1,128)S(1)}, u32[]{:S(2)}, u32[]{:S(2)}) collective-permute-start(f32[1,2304]{1,0:T(1,128)S(1)} %add.219), channel_id=1, source_target_pairs={{0,4},{2,6},{4,0},{6,2},{8,12},{10,14},{12,8},{14,10},{16,20},{18,... | collective-permute-start | bytes 27656 | tf_op jit(solution)/shard_map/ppermute | solution.py:315
  333.6 3.7 %collective-permute-start.12 = (f32[1,2304]{1,0:T(1,128)S(1)}, f32[1,2304]{1,0:T(1,128)S(1)}, u32[]{:S(2)}, u32[]{:S(2)}) collective-permute-start(f32[1,2304]{1,0:T(1,128)S(1)} %add.220), channel_id=1, source_target_pairs={{0,8},{2,10},{4,12},{6,14},{8,0},{10,2},{12,4},{14,6},{16,24},{18,... | collective-permute-start | bytes 27656 | tf_op jit(solution)/shard_map/ppermute | solution.py:315
  337.3 4.6 %collective-permute-start.13 = (f32[1,2304]{1,0:T(1,128)S(1)}, f32[1,2304]{1,0:T(1,128)S(1)}, u32[]{:S(2)}, u32[]{:S(2)}) collective-permute-start(f32[1,2304]{1,0:T(1,128)S(1)} %add.221), channel_id=1, source_target_pairs={{0,16},{2,18},{4,20},{6,22},{8,24},{10,26},{12,28},{14,30},{16,0},... | collective-permute-start | bytes 27656 | tf_op jit(solution)/shard_map/ppermute | solution.py:315
  (22 other events, 127.8 us)
